TPU v7x, 32 devices: a whole 2x2x4 slice. The times are simulated.
32 devices in a mesh: dp: 8 (over z, y), ctx: 4 (over x, core).
Axes of the slice: x: 2, y: 2, z: 4, core: 2. Of those that a mesh axis runs over, the one named last changes fastest.
Arguments:
- tokens: bfloat16 [8, 1024, 1024], P('dp', 'ctx'), may hold values from -6 to 6
- doc_ids: int32 [8, 1024], P('dp', 'ctx'), may hold values from 0 to 7, never falling along the last dimension, each value on 1 to 512 neighbouring positions
- w_query: bfloat16 [1024, 1024], P(('dp', 'ctx')), may hold values from -0.1875 to 0.1875
- key_weight: bfloat16 [1024, 512], P(('dp', 'ctx')), may hold values from -0.1875 to 0.1875
- value_weight: bfloat16 [1024, 512], P(('dp', 'ctx')), may hold values from -0.1875 to 0.1875
- w_output: bfloat16 [1024, 1024], P(None, ('dp', 'ctx')), may hold values from -1.5 to 1.5
- w_gate: bfloat16 [1024, 4608], P(('dp', 'ctx')), may hold values from -0.1875 to 0.1875
- w_up: bfloat16 [1024, 4608], P(('dp', 'ctx')), may hold values from -0.1875 to 0.1875
- w_down: bfloat16 [4608, 1024], P(None, ('dp', 'ctx')), may hold values from -0.09375 to 0.09375
- norm_gains: bfloat16 [2, 1024], P(None, ('dp', 'ctx')), may hold values from 0.5 to 1.5
- head_norm_gains: bfloat16 [2, 64], replicated, may hold values from 0.5 to 1.5
- out_grad: bfloat16 [8, 1024, 1024], P('dp', 'ctx'), may hold values from -6 to 6
Outputs:
- layer_out: bfloat16 [8, 1024, 1024], P('dp', 'ctx')
- input_grad: bfloat16 [8, 1024, 1024], P('dp', 'ctx')
- grad_query: bfloat16 [1024, 1024], P(('dp', 'ctx'))
- grad_key: bfloat16 [1024, 512], P(('dp', 'ctx'))
- grad_value: bfloat16 [1024, 512], P(('dp', 'ctx'))
- grad_output: bfloat16 [1024, 1024], P(None, ('dp', 'ctx'))
- grad_gate: bfloat16 [1024, 4608], P(('dp', 'ctx'))
- grad_up: bfloat16 [1024, 4608], P(('dp', 'ctx'))
- grad_down: bfloat16 [4608, 1024], P(None, ('dp', 'ctx'))
- grad_norms: bfloat16 [2, 1024], P(None, ('dp', 'ctx'))
- grad_heads: bfloat16 [2, 64], replicated
Inputs may be any that keep to these rules, and one draw needn't show every extreme that they name: `doc_ids`: along each sequence the numbers never fall; each document spans 1 to 512 tokens.
All inputs are finite; a program needn't handle non-finite values.
Results may differ from a plain program's by a relative error of at most 0.015.
Values may be sent and summed in bfloat16 or wider, within the bound.
No kernel may reach another device: no remote copies, remote signals or barrier semaphores. Data moves between devices by JAX's collectives and lax.ppermute only.
A program may use at most 320 MiB of HBM per device.

v0:
```python
import functools

import jax
import jax.numpy as jnp
from jax import lax
from jax.experimental import pallas as pl
from jax.experimental.pallas import tpu as pltpu
from jax.sharding import PartitionSpec as P

EPS = 1e-05
THETA = 1000000.0
BF = jnp.bfloat16
F32 = jnp.float32
ALL = ("dp", "ctx")


def add_low(*terms):
    total = terms[0].astype(F32)
    for term in terms[1:]:
        total = total + term.astype(F32)
    return total.astype(BF)


def flip(value, axis, size, bits):
    return lax.ppermute(value, axis, [(i, i ^ bits) for i in range(size)])


def gather_ctx(own):
    core = flip(own, "ctx", 4, 1)
    across = flip(own, "ctx", 4, 2)
    return [own, core, across, flip(across, "ctx", 4, 1)]


def scatter_ctx(parts):
    far = flip(parts[3], "ctx", 4, 1)
    near = flip(parts[1], "ctx", 4, 1)
    return parts[0], near, flip(add_low(parts[2], far), "ctx", 4, 2)


def sum_parts(parts):
    return parts[0].astype(F32) + parts[1].astype(F32) + parts[2].astype(F32)


def exchange_ctx(parts):
    return [parts[0]] + [flip(parts[j], "ctx", 4, j) for j in range(1, 4)]


def place(parts, where, axis):
    size = parts[0].shape[axis]
    shape = list(parts[0].shape)
    shape[axis] = size * len(parts)
    out = jnp.zeros(shape, parts[0].dtype)
    for part, at in zip(parts, where):
        out = lax.dynamic_update_slice_in_dim(out, part, at * size, axis)
    return out


def bar(*trees):
    return lax.optimization_barrier(trees)


def ordered(dp_size):
    return dp_size == 8


def dp_order(dp_size):
    me = lax.axis_index("dp")
    return [((me - 2 * (i % 4)) % dp_size) ^ (i // 4) for i in range(dp_size)]


def across_y(value):
    return flip(value, "dp", 8, 1)


def along_z(value):
    return lax.ppermute(value, "dp", [(i, (i + 2) % 8) for i in range(8)])


def sum_all(value, dp_size):
    for bits in (1, 2):
        value = value + flip(value, "ctx", 4, bits)
    bits = 1
    while bits < dp_size:
        value = value + flip(value, "dp", dp_size, bits)
        bits *= 2
    return value


def dot(a, b):
    return lax.dot_general(a, b, (((1,), (0,)), ((), ())), preferred_element_type=F32)


def dot_nt(a, b):
    return lax.dot_general(a, b, (((1,), (1,)), ((), ())), preferred_element_type=F32)


def dot_tn(a, b):
    return lax.dot_general(a, b, (((0,), (0,)), ((), ())), preferred_element_type=F32)


VMEM = pl.BlockSpec(memory_space=pltpu.VMEM)
SMEM = pl.BlockSpec(memory_space=pltpu.SMEM)
LANES = 128
HIGH = lax.Precision.HIGHEST


HEAVY = 10**11


def call(body, outs, ins, scratch=(), scalars=0, limit=4, flops=1000000, held=False):
    def spec(shape):
        if held:
            return VMEM
        zeros = (0,) * len(shape)
        return pl.BlockSpec(tuple(shape), lambda i: zeros, pipeline_mode=pl.Buffered(1))

    return pl.pallas_call(
        body,
        out_shape=[jax.ShapeDtypeStruct(shape, kind) for shape, kind in outs],
        grid=() if held else (1,),
        in_specs=[SMEM] * scalars + [spec(x.shape) for x in ins[scalars:]],
        out_specs=[spec(shape) for shape, _ in outs],
        scratch_shapes=list(scratch),
        compiler_params=pltpu.CompilerParams(vmem_limit_bytes=limit << 20),
        cost_estimate=pl.CostEstimate(flops=flops, bytes_accessed=1000, transcendentals=0),
    )(*ins)


def pack_body(order_ref, tokens_ref, docs_ref, out_ref):
    rows = tokens_ref.shape[0]

    def one(i, _):
        out_ref[:rows, columns(i, LANES)] = tokens_ref[:, columns(order_ref[i], LANES)]
        return 0

    lax.fori_loop(0, tokens_ref.shape[1] // LANES, one, 0)
    if docs_ref is not None:
        below = jnp.broadcast_to(docs_ref[...].astype(F32), (16, rows)).astype(BF)
        out_ref[rows:, :rows] = below
        out_ref[rows:, rows:] = jnp.zeros((16, out_ref.shape[1] - rows), BF)


def pack_rows(order, rows, doc_row=None):
    if doc_row is None:
        body = lambda order_ref, rows_ref, out_ref: pack_body(order_ref, rows_ref, None, out_ref)
        return call(body, [(rows.shape, BF)], [order, rows], scalars=1)[0]
    shape = (rows.shape[0] + 16, rows.shape[1])
    return call(pack_body, [(shape, BF)], [order, rows, doc_row.reshape(1, -1)], scalars=1)[0]


def sum_body(order_ref, base_ref, *refs):
    parts, out_ref = refs[:-1], refs[-1]

    def one(i, _):
        at = columns(i, LANES)
        total = base_ref[:, at]
        if parts:
            part = parts[0][:, at].astype(F32)
            for ref in parts[1:]:
                part = part + ref[:, at].astype(F32)
            total = total + part
        out_ref[:, columns(order_ref[i], LANES)] = total.astype(BF)
        return 0

    lax.fori_loop(0, base_ref.shape[1] // LANES, one, 0)


def sum_out(order, base, parts):
    return call(sum_body, [(base.shape, BF)], [order, base, *parts], scalars=1)[0]


def by_blocks(count, rows, body):
    def one(i, _):
        body(pl.ds(pl.multiple_of(i * rows, rows), rows))
        return 0

    lax.fori_loop(0, count, one, 0)


def move(target, to, source, start, rows):
    step = 32

    def one(i, _):
        goal = pl.ds(pl.multiple_of(to + i * step, step), step)
        target[goal, :] = source[pl.ds(pl.multiple_of(start + i * step, step), step), :]
        return 0

    lax.fori_loop(0, rows // step, one, 0)


def hand_out(ref, parts):
    rows = parts[0].shape[0]
    for j, part in enumerate(parts):
        move(part, 0, ref, j * rows, rows)


def lane_masks(rows):
    lane = lax.broadcasted_iota(jnp.int32, (rows, LANES), 1)
    return lane < 64, lax.rem(lane, 64) < 32


def half_sums(squares):
    row = lax.broadcasted_iota(jnp.int32, (LANES, LANES), 0) // 64
    col = lax.broadcasted_iota(jnp.int32, (LANES, LANES), 1) // 64
    return jnp.dot(
        squares, (row == col).astype(F32), preferred_element_type=F32, precision=HIGH
    )


def turn(value, first):
    return jnp.where(first, pltpu.roll(value, 96, 1), pltpu.roll(value, 32, 1))


def doubled(value, left):
    other = pltpu.roll(value, 64, 1)
    return jnp.where(left, value, other), jnp.where(left, other, value)


def prepare_body(rows, *refs):
    packs, blocks = refs[:4], refs[4:12]
    cos_ref, sin_ref, head_ref = refs[12:15]
    normed_ref, qk_pre_ref, q_ref, kd_ref, vd_ref, kt_ref, vt_ref = refs[15:22]
    wqkv_ref, wo_ref, gains_ref, all_ref = refs[22:26]
    for i, block in enumerate(blocks):
        at = i * LANES
        wqkv_ref[at : at + LANES, :] = block[:LANES, :512]
        wo_ref[at : at + LANES, :] = block[:LANES, 512:]
        gains_ref[:, at : at + LANES] = block[LANES : LANES + 8, :LANES].astype(F32)
    for j, pack in enumerate(packs):
        move(all_ref, j * rows, pack, 0, rows)
    left, first = lane_masks(LANES)
    gain = gains_ref[0:1, :]
    q_gain, k_gain = head_ref[0:1, :], head_ref[1:2, :]

    def chunk(i, _):
        at = pl.ds(pl.multiple_of(i * LANES, LANES), LANES)
        x = all_ref[at, :].astype(F32)
        scale = lax.rsqrt(jnp.mean(x * x, -1, keepdims=True) + EPS)
        normed = (x * scale * gain).astype(BF)
        normed_ref[at, :] = normed
        pre = jnp.dot(normed, wqkv_ref[...], preferred_element_type=F32)
        qk_pre_ref[at, :] = pre[:, :384]
        cos, sin = cos_ref[at, :], sin_ref[at, :]
        turned = []
        for b in range(3):
            u = pre[:, b * LANES : (b + 1) * LANES]
            u = u * lax.rsqrt(half_sums(u * u) * (1.0 / 64) + EPS) * (k_gain if b == 2 else q_gain)
            turned.append(u * cos + turn(u, first) * sin)
        q_ref[0, at, :] = turned[0].astype(BF)
        q_ref[1, at, :] = turned[1].astype(BF)
        key, value = turned[2], pre[:, 384:]
        for both, flat, one in ((kd_ref, kt_ref, key), (vd_ref, vt_ref, value)):
            low, high = doubled(one, left)
            both[0, at, :] = low.astype(BF)
            both[1, at, :] = high.astype(BF)
            flat[:, at] = one.T.astype(BF)
        return 0

    lax.fori_loop(0, all_ref.shape[0] // LANES, chunk, 0)


def two_heads(block, left):
    zero = jnp.zeros_like(block)
    return jnp.concatenate([jnp.where(left, block, zero), jnp.where(left, zero, block)], 0)


def seen(start_row, first_key, rows, first_query):
    shape = (rows, 2 * rows)
    key = lax.broadcasted_iota(jnp.int32, shape, 0)
    mask = key + first_key >= start_row
    if first_query is not None:
        lane = lax.broadcasted_iota(jnp.int32, shape, 1)
        mask = mask & (key <= jnp.where(lane < rows, lane, lane - rows))
    return mask


LOG2E = 1.4426950408889634
SCORE = LOG2E / 8.0


def attend_body(rows, me_ref, first_ref, q_ref, kd_ref, vt_ref, start_ref, wo_ref, *refs):
    parts = refs[:4]
    out_ref, wide_ref, lse_ref, sum_ref, acc_ref, part_ref = refs[4:10]
    me = me_ref[0]
    left = lax.broadcasted_iota(jnp.int32, (rows, LANES), 1) < 64

    def one(step, _):
        kv, a = step // 4, lax.rem(step, 4)
        at_q = pl.ds(pl.multiple_of((a ^ me) * rows, rows), rows)
        q2 = two_heads(q_ref[kv, at_q, :], left)
        start_row = start_ref[a ^ me]
        sum_ref[...] = jnp.zeros_like(sum_ref)
        acc_ref[...] = jnp.zeros_like(acc_ref)
        for d in range(3):

            @pl.when((a >= d) & (first_ref[a ^ me] < (a - d + 1) * rows))
            def _():
                at_k = pl.ds(pl.multiple_of(((a - d) ^ me) * rows, rows), rows)
                scores = dot_nt(kd_ref[kv, at_k, :], q2)
                mask = seen(start_row, (a - d) * rows, rows, a if d == 0 else None)
                p = jnp.where(mask, jnp.exp2(scores * SCORE), 0.0)
                sum_ref[...] += jnp.sum(p, 0, keepdims=True)
                half = pl.ds(pl.multiple_of(kv * 64, 64), 64)
                acc_ref[...] += dot(vt_ref[half, at_k], p.astype(BF))

        total = sum_ref[...]
        lse_ref[kv * 4 + (a ^ me)] = jnp.log2(total)
        mixed = acc_ref[...] / total
        mixed = jnp.concatenate([mixed[:, :rows], mixed[:, rows:]], 0).T
        wide_ref[kv, at_q, :] = mixed
        out_ref[at_q, columns(kv, LANES)] = mixed.astype(BF)
        return 0

    lax.fori_loop(0, 8, one, 0)

    def project(at):
        part_ref[at, :] = dot_nt(out_ref[at, :], wo_ref[...]).astype(BF)

    by_blocks(4, rows, project)
    hand_out(part_ref, parts)


def attend_back_body(rows, *refs):
    me_ref, first_ref = refs[:2]
    refs = refs[1:]
    g0, g1, g2, g3, q_ref, kd_ref, vd_ref, kt_ref, start_ref, wide_ref, lse_ref = refs[1:12]
    qk_pre_ref, cos_ref, sin_ref, head_ref, wqkv_ref, wo_ref, normed_ref, gains_ref = refs[12:20]
    parts, low_ref, head_sum_ref, gain_sum_ref, grad_ref = refs[20:24], *refs[24:28]
    mixed_ref, dq_ref, dk_ref, dv_ref, acc_ref = refs[28:33]
    me = me_ref[0]
    left = lax.broadcasted_iota(jnp.int32, (rows, LANES), 1) < 64
    for j, g in enumerate((g0, g1, g2, g3)):
        move(grad_ref, j * rows, g, 0, rows)

    def mix(at):
        grad = dot(grad_ref[at, :], wo_ref[...]).astype(BF)
        mixed_ref[0, at, :] = grad[:, :LANES]
        mixed_ref[1, at, :] = grad[:, LANES:]

    by_blocks(4, rows, mix)
    dk_ref[...] = jnp.zeros_like(dk_ref)
    dv_ref[...] = jnp.zeros_like(dv_ref)
    pick = (
        lax.broadcasted_iota(jnp.int32, (8, LANES), 1) // 64
        == lax.broadcasted_iota(jnp.int32, (8, LANES), 0)
    ).astype(F32)

    def one(step, _):
        kv, a = step // 4, lax.rem(step, 4)
        at_q = pl.ds(pl.multiple_of((a ^ me) * rows, rows), rows)
        q2 = two_heads(q_ref[kv, at_q, :], left)
        grad = mixed_ref[kv, at_q, :]
        g2 = two_heads(grad, left)
        inner = lax.dot_general(
            pick,
            grad.astype(F32) * wide_ref[kv, at_q, :],
            (((1,), (1,)), ((), ())),
            preferred_element_type=F32,
            precision=HIGH,
        )
        inner = jnp.concatenate([inner[0:1], inner[1:2]], 1)
        lse = lse_ref[kv * 4 + (a ^ me)]
        start_row = start_ref[a ^ me]
        acc_ref[...] = jnp.zeros_like(acc_ref)
        for d in range(3):

            @pl.when((a >= d) & (first_ref[a ^ me] < (a - d + 1) * rows))
            def _():
                at_k = pl.ds(pl.multiple_of(((a - d) ^ me) * rows, rows), rows)
                scores = dot_nt(kd_ref[kv, at_k, :], q2)
                mask = seen(start_row, (a - d) * rows, rows, a if d == 0 else None)
                p = jnp.where(mask, jnp.exp2(scores * SCORE - lse), 0.0)
                gp = dot_nt(vd_ref[kv, at_k, :], g2)
                gs = (p * (gp - inner)).astype(BF)
                dv_ref[kv, at_k, :] += dot(p.astype(BF), g2)
                dk_ref[kv, at_k, :] += dot(gs, q2)
                half = pl.ds(pl.multiple_of(kv * 64, 64), 64)
                acc_ref[...] += dot(kt_ref[half, at_k], gs)

        both = acc_ref[...] * 0.125
        dq_ref[kv, at_q, :] = jnp.concatenate([both[:, :rows], both[:, rows:]], 0).T
        return 0

    lax.fori_loop(0, 8, one, 0)
    left, first = lane_masks(LANES)
    head_sum_ref[...] = jnp.zeros_like(head_sum_ref)

    def folded(ref, at):
        low, high = ref[0, at, :], ref[1, at, :]
        low, high = low + pltpu.roll(low, 64, 1), high + pltpu.roll(high, 64, 1)
        return jnp.where(left, low, high)

    def chunk(i, _):
        at = pl.ds(pl.multiple_of(i * LANES, LANES), LANES)
        cos, sin = cos_ref[at, :], sin_ref[at, :]
        for b in range(3):
            u = qk_pre_ref[at, b * LANES : (b + 1) * LANES]
            g = folded(dk_ref, at) * 0.125 if b == 2 else dq_ref[b, at, :]
            w = g * cos - turn(g, first) * sin
            row = 1 if b == 2 else 0
            gain = head_ref[row : row + 1, :]
            r = lax.rsqrt(half_sums(u * u) * (1.0 / 64) + EPS)
            head_sum_ref[row : row + 1, :] += jnp.sum(w * u * r, 0, keepdims=True)
            w = w * gain
            back = r * w - u * (r * r * r) * (half_sums(w * u) * (1.0 / 64))
            low_ref[at, b * LANES : (b + 1) * LANES] = back.astype(BF)
        low_ref[at, 384:] = folded(dv_ref, at).astype(BF)
        return 0

    lax.fori_loop(0, low_ref.shape[0] // LANES, chunk, 0)
    gain_sum = jnp.zeros((1, normed_ref.shape[1]), F32)
    for j in range(4):
        at = slice(j * rows, (j + 1) * rows)
        grad = dot_nt(low_ref[at, :], wqkv_ref[...])
        parts[j][...] = grad.astype(BF)
        gain_sum = gain_sum + jnp.sum(grad * normed_ref[at, :].astype(F32), 0, keepdims=True)
    gain_sum_ref[...] = gain_sum / gains_ref[0:1, :]


def columns(at, width):
    return pl.ds(pl.multiple_of(at * width, LANES), width)


def spread_body(widths, me_ref, *refs):
    weights, outs = refs[: len(widths)], refs[-4:]
    rows = weights[0].shape[0]
    me = me_ref[0]
    for j, out in enumerate(outs):
        start = 0
        for weight, width in zip(weights, widths):
            out[:rows, start : start + width] = weight[:, columns(me ^ j, width)]
            start += width
    if len(refs) > len(widths) + 4:
        gains = refs[len(widths)][...].astype(F32)
        gains = jnp.concatenate([gains, jnp.zeros((6, rows), F32)], 0)
        gains = jnp.concatenate([gains] * (LANES // rows), 1)
        lane = lax.broadcasted_iota(jnp.int32, (8, LANES), 1)
        gains = jnp.where(lane // rows == me, gains, 0.0).astype(BF)
        for out in outs:
            out[rows:, :] = jnp.zeros((8, out.shape[1]), BF)
            out[rows:, :LANES] = gains


def join_body(rows, me_ref, *refs):
    pieces, out = refs[:4], refs[4]
    me = me_ref[0]
    for j, piece in enumerate(pieces):
        out[pl.ds(pl.multiple_of((me ^ j) * rows, rows), rows), :] = piece[:rows, :]
    if pieces[0].shape[0] > rows:
        below = [piece[rows:, :].astype(F32) for piece in pieces]
        out[4 * rows :, :] = (below[0] + below[1] + below[2] + below[3]).astype(BF)


def part_body(me_ref, one_ref, two_ref, three_ref, *refs):
    outs, total_ref = refs[:4], refs[4]
    total = one_ref[...].astype(F32) + two_ref[...].astype(F32) + three_ref[...].astype(F32)
    total_ref[...] = total
    rows = outs[0].shape[0]
    for j, out in enumerate(outs):
        at = pl.ds(pl.multiple_of((me_ref[0] ^ j) * rows, rows), rows)
        out[...] = total_ref[at, :].astype(BF)


def land_body(widths, me_ref, *refs):
    pieces, outs = refs[:4], refs[4:]
    me = me_ref[0]
    start = 0
    for out, width in zip(outs, widths):
        for j, piece in enumerate(pieces):
            out[:, columns(me ^ j, width)] = piece[:, start : start + width]
        start += width


def small_body(order_ref, one_ref, two_ref, head_ref, *refs):
    out_ref = refs[-1]
    out_ref[...] = jnp.zeros_like(out_ref)
    for i in range(one_ref.shape[1] // LANES):
        at = columns(order_ref[i], LANES)
        out_ref[0:1, at] = one_ref[:, i * LANES : (i + 1) * LANES]
        out_ref[1:2, at] = two_ref[:, i * LANES : (i + 1) * LANES]
    out_ref[2:4, :LANES] = head_ref[0:2, :]


def feed_body(rows, pieces, *refs):
    normed, packs, weights = refs[:4], refs[4:8], refs[8 : 8 + pieces]
    hidden_ref, gate_ref, up_ref, w_ref, down_ref, normed_ref, grad_ref = refs[8 + pieces :]
    ff = hidden_ref.shape[1]
    row = 0
    for weight in weights:
        move(w_ref, row, weight.at[:, : 2 * ff], 0, weight.shape[0])
        move(down_ref, row, weight.at[:, 2 * ff :], 0, weight.shape[0])
        row += weight.shape[0]
    for j in range(4):
        move(normed_ref, j * rows, normed[j], 0, rows)
        move(grad_ref, j * rows, packs[j], 0, rows)

    def one(i, _):
        at = pl.ds(pl.multiple_of(i * rows, rows), rows)
        x = normed_ref[at, :]
        gate, up = dot(x, w_ref[:, :ff]), dot(x, w_ref[:, ff:])
        grad = dot(grad_ref[at, :], down_ref[...])
        sig = 1.0 / (1.0 + jnp.exp(-gate))
        silu = gate * sig
        hidden_ref[at, :] = (silu * up).astype(BF)
        gate_ref[at, :] = (grad * up * (sig * (1.0 + gate * (1.0 - sig)))).astype(BF)
        up_ref[at, :] = (grad * silu).astype(BF)
        return 0

    lax.fori_loop(0, 4, one, 0)


def feed_back_body(rows, gate_ref, up_ref, w_ref, *refs):
    parts, part_ref = refs[:4], refs[4]
    ff = gate_ref.shape[1]

    def one(i, _):
        at = pl.ds(pl.multiple_of(i * rows, rows), rows)
        total = dot_nt(gate_ref[at, :], w_ref[:, :ff]) + dot_nt(up_ref[at, :], w_ref[:, ff:])
        part_ref[at, :] = total.astype(BF)
        return 0

    lax.fori_loop(0, 4, one, 0)
    hand_out(part_ref, parts)


def down_body(rows, hidden_ref, down_ref, *refs):
    parts, part_ref = refs[:4], refs[4]

    def one(at):
        part_ref[at, :] = dot_nt(hidden_ref[at, :], down_ref[...]).astype(BF)

    by_blocks(4, rows, one)
    hand_out(part_ref, parts)


def attn_weights_body(normed_ref, grad_qkv_ref, grad_ref, out_ref, *chunks):
    cut = grad_qkv_ref.shape[1]
    chunks, whole_ref = chunks[:-1], chunks[-1]
    width = 2 * LANES

    def one(i, _):
        at = columns(i, width)
        whole_ref[at, :cut] = dot_tn(normed_ref[:, at], grad_qkv_ref[...]).astype(BF)
        whole_ref[at, cut:] = dot_tn(grad_ref[:, at], out_ref[...]).astype(BF)
        return 0

    lax.fori_loop(0, whole_ref.shape[0] // width, one, 0)
    hand_out(whole_ref, chunks)


def rms_scale(values, gain_row):
    return values * lax.rsqrt(jnp.mean(values * values, -1, keepdims=True) + EPS) * gain_row


def place_all(pieces, me, widths):
    outs, start = [], 0
    for width in widths:
        cut = [p[:, start : start + width] for p in pieces]
        outs.append(place(cut, [me ^ j for j in range(4)], 1))
        start += width
    return outs


def on_device(
    dp_size,
    tokens,
    doc_ids,
    w_query,
    key_weight,
    value_weight,
    w_output,
    w_gate,
    w_up,
    w_down,
    norm_gains,
    head_norm_gains,
    out_grad,
):
    local_len, model_dim = tokens.shape[1:]
    tokens, out_grad, doc_row = tokens[0], out_grad[0], doc_ids[0]
    head_dim = head_norm_gains.shape[1]
    q_cols, kv_cols = w_query.shape[1] // 4, key_weight.shape[1] // 4
    shard = norm_gains.shape[1]
    ff_cols = w_gate.shape[1] // 4
    me = lax.axis_index("ctx")
    places = [me ^ j for j in range(4)]
    full_len = 4 * local_len
    fast = ordered(dp_size)
    block_order = jnp.stack(dp_order(dp_size)) if fast else jnp.arange(model_dim // LANES)
    block_order = block_order.astype(jnp.int32)
    me_row = me.reshape(1).astype(jnp.int32)
    attn_widths = (q_cols, kv_cols, kv_cols, q_cols)
    ff_widths = (ff_cols, ff_cols, ff_cols)
    wide, ff_wide = sum(attn_widths), sum(ff_widths)
    attn_local = [w_query, key_weight, value_weight, w_output.T]
    ff_local = [w_gate, w_up, w_down.T]

    pack = pack_rows(block_order, tokens, doc_row)
    grad_pack = pack_rows(block_order, out_grad)
    if fast:
        sent = call(
            functools.partial(spread_body, attn_widths),
            [((shard + 8, wide), BF)] * 4,
            [me_row, *attn_local, norm_gains],
            scalars=1,
        )
        ff_sent = call(
            functools.partial(spread_body, ff_widths),
            [((shard, ff_wide), BF)] * 4,
            [me_row, *ff_local],
            scalars=1,
        )
        got, ff_sent = bar(exchange_ctx(sent), ff_sent)
        ff_got = exchange_ctx(ff_sent)
        (block,) = call(
            functools.partial(join_body, shard),
            [((4 * shard + 8, wide), BF)],
            [me_row, *got],
            scalars=1,
        )
        y0, z1, pack, ff_got = bar(across_y(block), along_z(block), pack, ff_got)
        core_pack, far_pack = flip(pack, "ctx", 4, 1), flip(pack, "ctx", 4, 2)
        y1, z2 = bar(across_y(z1), along_z(z1))
        (ff_block,) = call(
            functools.partial(join_body, shard),
            [((4 * shard, ff_wide), BF)],
            [me_row, *ff_got],
            scalars=1,
        )
        y2, z3, far_pack, grad_pack, ff_block = bar(
            across_y(z2), along_z(z2), far_pack, grad_pack, ff_block
        )
        far_core_pack = flip(far_pack, "ctx", 4, 1)
        y3, ff_block, far_core_pack = bar(across_y(z3), ff_block, far_core_pack)
        ff_z1, ff_y0 = along_z(ff_block), across_y(ff_block)
        blocks = [block, z1, z2, z3, y0, y1, y2, y3]
    else:

        def pieces_of(weights):
            sent = []
            for at in places:
                cut = [
                    lax.dynamic_slice_in_dim(w, at * (w.shape[1] // 4), w.shape[1] // 4, 1)
                    for w in weights
                ]
                sent.append(jnp.concatenate(cut, 1))
            return sent

        def whole(weights):
            block = place(exchange_ctx(pieces_of(weights)), places, 0)
            return lax.all_gather(block, "dp", axis=0, tiled=True)

        gains = lax.all_gather(norm_gains, ALL, axis=1, tiled=True).reshape(2, -1, LANES)
        gains = jnp.pad(gains.transpose(1, 0, 2), ((0, 0), (0, 6), (0, wide - LANES)))
        blocks = jnp.concatenate([whole(attn_local).reshape(-1, LANES, wide), gains], 1)
        blocks = [blocks[i] for i in range(blocks.shape[0])]
        ff_w = [whole(ff_local)]
        core_pack, far_pack = flip(pack, "ctx", 4, 1), flip(pack, "ctx", 4, 2)
        far_core_pack = flip(far_pack, "ctx", 4, 1)

    packs = [pack, core_pack, far_pack, far_core_pack]
    core_grad, far_grad = flip(grad_pack, "ctx", 4, 1), flip(grad_pack, "ctx", 4, 2)
    docs = jnp.concatenate([p[local_len, :local_len] for p in packs])
    index = jnp.concatenate(
        [at * local_len + jnp.arange(local_len, dtype=jnp.int32) for at in places]
    )
    starts = jnp.sum((docs[None, :] < docs[:, None]).astype(jnp.int32), -1)
    positions = (index - starts).astype(F32)
    half = head_dim // 2
    lane = jnp.arange(LANES)
    freqs = THETA ** (-(2.0 * (lane % half).astype(F32)) / head_dim)
    angles = positions[:, None] * freqs
    cosine = jnp.cos(angles)
    sine = jnp.sin(angles) * jnp.where(lane % head_dim < half, -1.0, 1.0)
    starts = starts.reshape(4, local_len)
    firsts = starts[:, 0]
    starts = jnp.concatenate([starts, starts], 1).reshape(4, 1, 2 * local_len)
    head_gains = jnp.concatenate([head_norm_gains, head_norm_gains], 1).astype(F32)

    part_shapes = [((local_len, model_dim), BF)] * 4
    normed_one, qk_pre, queries, keys, values, keys_t, values_t, w_qkv, wo_t, gains = call(
        functools.partial(prepare_body, local_len),
        [
            ((full_len, model_dim), BF),
            ((full_len, q_cols + kv_cols), F32),
            ((2, full_len, LANES), BF),
            ((2, full_len, LANES), BF),
            ((2, full_len, LANES), BF),
            ((LANES, full_len), BF),
            ((LANES, full_len), BF),
            ((model_dim, q_cols + 2 * kv_cols), BF),
            ((model_dim, q_cols), BF),
            ((8, model_dim), F32),
        ],
        [*packs, *blocks, cosine, sine, head_gains],
        [pltpu.VMEM((full_len, model_dim), BF)],
        limit=28,
        flops=HEAVY,
    )
    if fast:
        queries, keys, ff_z1, ff_y0, core_grad, far_grad = bar(
            queries, keys, ff_z1, ff_y0, core_grad, far_grad
        )
        ff_z2, ff_y1 = along_z(ff_z1), across_y(ff_z1)
    grad_packs = [grad_pack, core_grad, far_grad, flip(far_grad, "ctx", 4, 1)]
    *resid_parts, attn_out, attn_wide, lse = call(
        functools.partial(attend_body, local_len),
        part_shapes
        + [
            ((full_len, q_cols), BF),
            ((2, full_len, LANES), F32),
            ((8, 1, 2 * local_len), F32),
        ],
        [me_row, firsts, queries, keys, values_t, starts, wo_t],
        [
            pltpu.VMEM((1, 2 * local_len), F32),
            pltpu.VMEM((head_dim, 2 * local_len), F32),
            pltpu.VMEM((full_len, model_dim), BF),
        ],
        scalars=2,
        limit=20,
    )
    own_tokens = pack[:local_len].astype(F32)
    own_grad = grad_pack.astype(F32)
    near_one, far_one = flip(resid_parts[1], "ctx", 4, 1), flip(resid_parts[3], "ctx", 4, 1)
    far_one = add_low(resid_parts[2], far_one)
    if fast:
        far_one, ff_z2, ff_y1 = bar(far_one, ff_z2, ff_y1)
        ff_z3, ff_y2 = along_z(ff_z2), across_y(ff_z2)
    far_one = flip(far_one, "ctx", 4, 2)
    resid = own_tokens + sum_parts((resid_parts[0], near_one, far_one))
    normed_own = rms_scale(resid, gains[1]).astype(BF)
    normed_core, normed_far = flip(normed_own, "ctx", 4, 1), flip(normed_own, "ctx", 4, 2)
    if fast:
        normed_far, ff_z3, ff_y2 = bar(normed_far, ff_z3, ff_y2)
        cut = ff_block.shape[0] // 2
        ff_w = [ff_block, ff_z1, ff_z2, ff_z3, ff_y0, ff_y1, ff_y2]
        ff_w += [across_y(ff_z3[:cut]), along_z(ff_y2[cut:])]
    normed_two = [normed_own, normed_core, normed_far, flip(normed_far, "ctx", 4, 1)]

    ff_shape = ((full_len, ff_cols), BF)
    hidden, grad_gate, grad_up, w_own, w_down_own, normed_all, grad_all = call(
        functools.partial(feed_body, local_len, len(ff_w)),
        [ff_shape] * 3
        + [((model_dim, 2 * ff_cols), BF), ((model_dim, ff_cols), BF)]
        + [((full_len, model_dim), BF)] * 2,
        [*normed_two, *grad_packs, *ff_w],
        limit=16,
        held=True,
    )

    def ff_chunks(at):
        cut = [dot_tn(normed_all[:, at], g).astype(BF) for g in (grad_gate, grad_up)]
        cut.append(dot_tn(grad_all[:, at], hidden).astype(BF))
        rows = cut[0].shape[0] // 4
        return [
            jnp.concatenate([c[r * rows : (r + 1) * rows] for c in cut], 1) for r in range(4)
        ]

    def pieces_of_sum(last):
        wide = last[0].shape[1]
        return call(
            part_body,
            [((shard, wide), BF)] * 4,
            [me_row, *last],
            [pltpu.VMEM((4 * shard, wide), F32)],
            scalars=1,
            limit=12,
        )

    def land(pieces, widths):
        return call(
            functools.partial(land_body, widths),
            [((shard, 4 * width), BF) for width in widths],
            [me_row, *pieces],
            scalars=1,
        )

    def plain_sums(chunks, widths):
        mine = lax.psum_scatter(jnp.concatenate(chunks, 0), "dp", scatter_dimension=0, tiled=True)
        pieces = [lax.dynamic_slice_in_dim(mine, at * shard, shard, 0) for at in places]
        return place_all(exchange_ctx(pieces), me, widths)

    def tick(*values):
        def body(*refs):
            refs[-1][...] = jnp.zeros((8, LANES), BF)

        return pl.pallas_call(
            body,
            out_shape=jax.ShapeDtypeStruct((8, LANES), BF),
            in_specs=[pl.BlockSpec(memory_space=pl.ANY)] * len(values),
            out_specs=VMEM,
            cost_estimate=pl.CostEstimate(flops=HEAVY, bytes_accessed=1000, transcendentals=0),
        )(*values)

    middle = model_dim // 2
    far = ff_chunks(slice(middle, None))
    if fast:
        cut = 4 * shard // 2
        first, early = across_y(far[1][:cut]), along_z(far[1][cut:])
        far[1], grad_gate, grad_up = bar(far[1], grad_gate, grad_up)
    *two_parts, = call(
        functools.partial(feed_back_body, local_len),
        part_shapes,
        [grad_gate, grad_up, w_own],
        [pltpu.VMEM((full_len, model_dim), BF)],
        limit=8,
        held=True,
    )
    near_two, far_two = flip(two_parts[1], "ctx", 4, 1), flip(two_parts[3], "ctx", 4, 1)
    if fast:
        near_two, far_two, hidden, normed_all, grad_all = bar(near_two, far_two, hidden, normed_all, grad_all)
    near = ff_chunks(slice(0, middle))
    far_two = add_low(two_parts[2], far_two)
    if fast:
        second = jnp.concatenate([far[2][:cut], add_low(far[2][cut:], early)], 0)
        total = jnp.concatenate([add_low(near[1][:cut], first), near[1][cut:]], 0)
        far_two, total, second = bar(far_two, total, second)
        total, second = along_z(total), across_y(second)
    far_two = flip(far_two, "ctx", 4, 2)
    grad_norm_two = sum_parts((two_parts[0], near_two, far_two))
    _, second_pull = jax.vjp(rms_scale, resid, gains[1])
    grad_resid_norm, grad_gain_two = second_pull(grad_norm_two)
    grad_resid = own_grad + grad_resid_norm
    (*down_parts,) = call(
        functools.partial(down_body, local_len),
        part_shapes,
        [hidden, w_down_own],
        [pltpu.VMEM((full_len, model_dim), BF)],
        limit=18,
    )

    grad_low = grad_resid.astype(BF)
    grad_core, grad_far = flip(grad_low, "ctx", 4, 1), flip(grad_low, "ctx", 4, 2)
    if fast:
        grad_far, down_parts = bar(grad_far, down_parts)
    down_near, down_far = flip(down_parts[1], "ctx", 4, 1), flip(down_parts[3], "ctx", 4, 1)
    down_far = add_low(down_parts[2], down_far)
    grad_attn = [grad_low, grad_core, grad_far, flip(grad_far, "ctx", 4, 1)]
    if fast:
        total, third = bar(add_low(near[2], second, total), far[3])
        grad_attn, down_far, tick_two = bar(grad_attn, down_far, tick(total))
        total, third = along_z(total), across_y(third)
    down_far = flip(down_far, "ctx", 4, 2)
    *one_parts, grad_qkv, head_sums, gain_one, grad_attn_all = call(
        functools.partial(attend_back_body, local_len),
        part_shapes
        + [
            ((full_len, q_cols + 2 * kv_cols), BF),
            ((8, LANES), F32),
            ((1, model_dim), F32),
            ((full_len, model_dim), BF),
        ],
        [
            me_row,
            firsts,
            *grad_attn,
            queries,
            keys,
            values,
            keys_t,
            starts,
            attn_wide,
            lse,
            qk_pre,
            cosine,
            sine,
            head_gains,
            w_qkv,
            wo_t,
            normed_one,
            gains,
        ],
        [
            pltpu.VMEM((2, full_len, LANES), BF),
            pltpu.VMEM((2, full_len, LANES), F32),
            pltpu.VMEM((2, full_len, LANES), F32),
            pltpu.VMEM((2, full_len, LANES), F32),
            pltpu.VMEM((head_dim, 2 * local_len), F32),
        ],
        scalars=2,
        limit=24,
        held=True,
    )
    if fast:
        fourth, grad_qkv = bar(far[0], grad_qkv)
        fourth = across_y(fourth)
        total, grad_qkv = bar(add_low(near[3], third, total), grad_qkv)
        last = (near[0], fourth, along_z(total))
    layer_out = sum_out(block_order, resid, (down_parts[0], down_near, down_far))
    attn_chunks = call(
        attn_weights_body,
        [((LANES, wide), BF)] * 8,
        [normed_one, grad_qkv, grad_attn_all, attn_out],
        [pltpu.VMEM((model_dim, wide), BF)],
        limit=20,
    )
    ticks = [tick_two] if fast else []
    (small,) = call(
        small_body,
        [((4, model_dim), F32)],
        [block_order, gain_one, grad_gain_two.reshape(1, -1), head_sums, *ticks],
        scalars=1,
    )
    grad_one = scatter_ctx(one_parts)
    if fast:
        near, far = attn_chunks[:4], attn_chunks[4:]
        total, last = bar(add_low(near[1], across_y(far[1])), last)
        ff_pieces = pieces_of_sum(last)
        total, small_core = bar(
            add_low(near[2], across_y(far[2]), along_z(total)), flip(small, "ctx", 4, 1)
        )
        small = small + small_core
        small = small + flip(small, "ctx", 4, 2)
        total, small_y = bar(
            add_low(near[3], across_y(far[3]), along_z(total)), flip(small, "dp", dp_size, 1)
        )
        small = small + small_y
        attn_last = (near[0], across_y(far[0]), along_z(total))
        attn_last, small_z, ff_got = bar(
            attn_last, flip(small, "dp", dp_size, 2), exchange_ctx(ff_pieces)
        )
        small = small + small_z
        small = small + flip(small, "dp", dp_size, 4)
        attn_pieces = exchange_ctx(pieces_of_sum(attn_last))
        grad_g_out, grad_u_out, grad_d_out = land(ff_got, ff_widths)
        grad_q_out, grad_k_out, grad_v_out, grad_o_out = land(attn_pieces, attn_widths)
    else:
        grad_g_out, grad_u_out, grad_d_out = plain_sums(near + far, ff_widths)
        grad_q_out, grad_k_out, grad_v_out, grad_o_out = plain_sums(attn_chunks, attn_widths)
        small = sum_all(small, dp_size)
    _, first_pull = jax.vjp(lambda u: rms_scale(u, gains[0]), own_tokens)
    input_grad = sum_out(block_order, grad_resid + first_pull(sum_parts(grad_one))[0], ())
    norm_own = lax.dynamic_slice_in_dim(small[:2], lax.axis_index(ALL) * shard, shard, 1)
    head_sum = small[2:, :head_dim] + small[2:, head_dim : 2 * head_dim]
    return (
        layer_out[None],
        input_grad[None],
        grad_q_out,
        grad_k_out,
        grad_v_out,
        grad_o_out.T,
        grad_g_out,
        grad_u_out,
        grad_d_out.T,
        norm_own.astype(BF),
        head_sum.astype(BF),
    )


def solution(mesh):
    def step(*arrays):
        return on_device(mesh.shape["dp"], *arrays)

    in_specs = (
        P("dp", "ctx", None),
        P("dp", "ctx"),
        P(("dp", "ctx"), None),
        P(("dp", "ctx"), None),
        P(("dp", "ctx"), None),
        P(None, ("dp", "ctx")),
        P(("dp", "ctx"), None),
        P(("dp", "ctx"), None),
        P(None, ("dp", "ctx")),
        P(None, ("dp", "ctx")),
        P(),
        P("dp", "ctx", None),
    )
    out_specs = (
        P("dp", "ctx", None),
        P("dp", "ctx", None),
        P(("dp", "ctx"), None),
        P(("dp", "ctx"), None),
        P(("dp", "ctx"), None),
        P(None, ("dp", "ctx")),
        P(("dp", "ctx"), None),
        P(("dp", "ctx"), None),
        P(None, ("dp", "ctx")),
        P(None, ("dp", "ctx")),
        P(),
    )
    return jax.shard_map(step, mesh=mesh, in_specs=in_specs, out_specs=out_specs, check_vma=False)
```

profile of v0, /device:TPU:0, one launch (start us, length us, event | category | flops | bytes accessed | tf_op | source)
XLA Modules:
  0.0 307.3 jit_solution(11480710491574975633)
XLA Ops:
  18.3 4.9 %collective-permute-done.4.refs_5_ = bf16[136,768]{1,0:T(8,128)(2,1)S(1)} collective-permute-done((bf16[136,768]{1,0:T(8,128)(2,1)S(1)}, bf16[136,768]{1,0:T(8,128)(2,1)S(1)}, u32[]{:S(2)}, u32[]{:S(2)}) %collective-permute-start.4) | collective-permute-done | bytes 208928 | tf_op jit(solution)/shard_map/ppermute | solution.py:76
  29.7 4.6 %collective-permute-done.10.refs_6_ = bf16[136,768]{1,0:T(8,128)(2,1)S(1)} collective-permute-done((bf16[136,768]{1,0:T(8,128)(2,1)S(1)}, bf16[136,768]{1,0:T(8,128)(2,1)S(1)}, u32[]{:S(2)}, u32[]{:S(2)}) %collective-permute-start.10) | collective-permute-done | bytes 208928 | tf_op jit(solution)/shard_map/ppermute | solution.py:76
  37.8 5.0 %collective-permute-done.12.refs_7_ = bf16[136,768]{1,0:T(8,128)(2,1)S(1)} collective-permute-done((bf16[136,768]{1,0:T(8,128)(2,1)S(1)}, bf16[136,768]{1,0:T(8,128)(2,1)S(1)}, u32[]{:S(2)}, u32[]{:S(2)}) %collective-permute-start.12) | collective-permute-done | bytes 208928 | tf_op jit(solution)/shard_map/ppermute | solution.py:76
  46.1 5.0 %collective-permute-done.14.refs_11_ = bf16[136,768]{1,0:T(8,128)(2,1)S(1)} collective-permute-done((bf16[136,768]{1,0:T(8,128)(2,1)S(1)}, bf16[136,768]{1,0:T(8,128)(2,1)S(1)}, u32[]{:S(2)}, u32[]{:S(2)}) %collective-permute-start.14) | collective-permute-done | bytes 208928 | tf_op jit(solution)/shard_map/ppermute | solution.py:25
  58.2 8.3 %shard_map.209 = (bf16[1024,1024]{1,0:T(8,128)(2,1)S(1)}, f32[1024,384]{1,0:T(8,128)S(1)}, bf16[2,1024,128]{2,1,0:T(8,128)(2,1)S(1)}, bf16[2,1024,128]{2,1,0:T(8...) custom-call(bf16[272,1024]{1,0:T(8,128)(2,1)S(1)} %shard_map.206.ref, ...), custom_call_target="tpu_custom_call" | custom-call | flops 99999997952 | bytes 1000 | tf_op jit(solution)/shard_map/pallas_call | solution.py:117
  79.3 9.5 %shard_map.210 = (bf16[256,1024]{1,0:T(8,128)(2,1)S(1)}, bf16[256,1024]{1,0:T(8,128)(2,1)S(1)}, bf16[256,1024]{1,0:T(8,128)(2,1)S(1)}, bf16[256,1024]{1,0:T(8,12...) custom-call(s32[1]{0:T(128)} %bitcast.8.me_ref.refs_0_, ...), custom_call_target="tpu_custom_call" | custom-call | flops 1000000 | bytes 1000 | tf_op jit(solution)/shard_map/pallas_call | solution.py:117
  91.0 4.8 %collective-permute-done.23.refs_13_ = bf16[128,3456]{1,0:T(8,128)(2,1)S(1)} collective-permute-done((bf16[128,3456]{1,0:T(8,128)(2,1)}, bf16[128,3456]{1,0:T(8,128)(2,1)S(1)}, u32[]{:S(2)}, u32[]{:S(2)}) %collective-permute-start.23) | collective-permute-done | bytes 884768 | tf_op jit(solution)/shard_map/ppermute | solution.py:25
  100.9 8.2 %collective-permute-done.24 = bf16[256,1024]{1,0:T(8,128)(2,1)S(1)} collective-permute-done((bf16[256,1024]{1,0:T(8,128)(2,1)S(1)}, bf16[256,1024]{1,0:T(8,128)(2,1)S(1)}, u32[]{:S(2)}, u32[]{:S(2)}) %collective-permute-start.24) | collective-permute-done | bytes 524320 | tf_op jit(solution)/shard_map/ppermute | solution.py:25
  112.0 5.9 %collective-permute-done.28.refs_14_ = bf16[128,3456]{1,0:T(8,128)(2,1)S(1)} collective-permute-done((bf16[128,3456]{1,0:T(8,128)(2,1)S(1)}, bf16[128,3456]{1,0:T(8,128)(2,1)S(1)}, u32[]{:S(2)}, u32[]{:S(2)}) %collective-permute-start.28) | collective-permute-done | bytes 884768 | tf_op jit(solution)/shard_map/ppermute | solution.py:25
  117.8 3.0 collective-permute-done.27.refs_11_
  122.0 13.5 %collective-permute-done.32.refs_16_ = bf16[64,3456]{1,0:T(8,128)(2,1)S(1)} collective-permute-done((bf16[64,3456]{1,0:T(8,128)(2,1)S(1)}, bf16[64,3456]{1,0:T(8,128)(2,1)S(1)}, u32[]{:S(2)}, u32[]{:S(2)}) %collective-permute-start.32) | collective-permute-done | bytes 442400 | tf_op jit(solution)/shard_map/ppermute | solution.py:76
  135.6 13.0 %shard_map.211 = (bf16[1024,1152]{1,0:T(8,128)(2,1)S(1)}, bf16[1024,1152]{1,0:T(8,128)(2,1)S(1)}, bf16[1024,1152]{1,0:T(8,128)(2,1)S(1)}, bf16[1024,2304]{1,0:T(...) custom-call(bf16[256,1024]{1,0:T(8,128)(2,1)S(1)} %multiply_convert_, ...), custom_call_target="tpu_custom_call" | custom-call | flops 1000000 | bytes 1000 | tf_op jit(solution)/shard_map/pallas_call | solution.py:117
  154.2 6.4 %shard_map.212 = (bf16[256,1024]{1,0:T(8,128)(2,1)S(1)}, bf16[256,1024]{1,0:T(8,128)(2,1)S(1)}, bf16[256,1024]{1,0:T(8,128)(2,1)S(1)}, bf16[256,1024]{1,0:T(8,128)(2,1)S(1)}) custom-call(bf16[1024,1152]{1,0:T(8,128)(2,1)S(1)} %get-tuple-element.221.gate_ref, bf16[1024,1152]{1,0:T(8,128)(2,1)S(1)} %get-tuple-element.222.up_ref, ...), custom_call_target="tpu_custom_call" | custom-call | flops 1000000 | bytes 1000 | tf_op jit(solution)/shard_map/pallas_call | solution.py:117
  162.0 5.7 %collective-permute-done.36 = bf16[64,3456]{1,0:T(8,128)(2,1)S(1)} collective-permute-done((bf16[64,3456]{1,0:T(8,128)(2,1)S(1)}, bf16[64,3456]{1,0:T(8,128)(2,1)S(1)}, u32[]{:S(2)}, u32[]{:S(2)}) %collective-permute-start.36) | collective-permute-done | bytes 442400 | tf_op jit(solution)/shard_map/ppermute | solution.py:76
  180.3 4.5 %shard_map.213 = (bf16[256,1024]{1,0:T(8,128)(2,1)S(1)}, bf16[256,1024]{1,0:T(8,128)(2,1)S(1)}, bf16[256,1024]{1,0:T(8,128)(2,1)S(1)}, bf16[256,1024]{1,0:T(8,128)(2,1)}) custom-call(bf16[1024,1152]{1,0:T(8,128)(2,1)S(1)} %get-tuple-element.232.hidden_ref, bf16[1024,1152]{1,0:T(8,128)(2,1)S(1)} %get-tuple-element.234.down_ref), custom_call_target="tpu_custom_call" | custom-call | flops 1000000 | bytes 1000 | tf_op jit(solution)/shard_map/pallas_call | solution.py:117
  184.8 3.8 %collective-permute-done.37 = bf16[256,1024]{1,0:T(8,128)(2,1)S(1)} collective-permute-done((bf16[256,1024]{1,0:T(8,128)(2,1)S(1)}, bf16[256,1024]{1,0:T(8,128)(2,1)S(1)}, u32[]{:S(2)}, u32[]{:S(2)}) %collective-permute-start.37) | collective-permute-done | bytes 524320 | tf_op jit(solution)/shard_map/ppermute | solution.py:25
  192.6 5.2 %collective-permute-done.43 = bf16[128,3456]{1,0:T(8,128)(2,1)S(1)} collective-permute-done((bf16[128,3456]{1,0:T(8,128)(2,1)S(1)}, bf16[128,3456]{1,0:T(8,128)(2,1)S(1)}, u32[]{:S(2)}, u32[]{:S(2)}) %collective-permute-start.43) | collective-permute-done | bytes 884768 | tf_op jit(solution)/shard_map/ppermute | solution.py:25
  202.6 3.8 %collective-permute-done.38.refs_4_ = bf16[256,1024]{1,0:T(8,128)(2,1)} collective-permute-done((bf16[256,1024]{1,0:T(8,128)(2,1)}, bf16[256,1024]{1,0:T(8,128)(2,1)}, u32[]{:S(2)}, u32[]{:S(2)}) %collective-permute-start.38) | collective-permute-done | bytes 524320 | tf_op jit(solution)/shard_map/ppermute | solution.py:25
  218.0 19.9 %shard_map.216 = (bf16[256,1024]{1,0:T(8,128)(2,1)S(1)}, bf16[256,1024]{1,0:T(8,128)(2,1)}, bf16[256,1024]{1,0:T(8,128)(2,1)S(1)}, bf16[256,1024]{1,0:T(8,128)(2...) custom-call(s32[1]{0:T(128)} %bitcast.8.me_ref.refs_0_, ...), custom_call_target="tpu_custom_call" | custom-call | flops 1000000 | bytes 1000 | tf_op jit(solution)/shard_map/pallas_call | solution.py:117
  242.3 3.6 %shard_map.218 = (bf16[128,768]{1,0:T(8,128)(2,1)S(1)}, bf16[128,768]{1,0:T(8,128)(2,1)S(1)}, bf16[128,768]{1,0:T(8,128)(2,1)S(1)}, bf16[128,768]{1,0:T(8,128)(2...) custom-call(bf16[1024,1024]{1,0:T(8,128)(2,1)S(1)} %get-tuple-elemen, ...), custom_call_target="tpu_custom_call" | custom-call | flops 1000000 | bytes 1000 | tf_op jit(solution)/shard_map/pallas_call | solution.py:117
  248.7 15.4 %collective-permute-done.54 = bf16[128,768]{1,0:T(8,128)(2,1)S(1)} collective-permute-done((bf16[128,768]{1,0:T(8,128)(2,1)S(1)}, bf16[128,768]{1,0:T(8,128)(2,1)S(1)}, u32[]{:S(2)}, u32[]{:S(2)}) %collective-permute-start.54) | collective-permute-done | bytes 196640 | tf_op jit(solution)/shard_map/ppermute | solution.py:25
  284.9 3.3 %collective-permute-done.59 = bf16[128,768]{1,0:T(8,128)(2,1)S(1)} collective-permute-done((bf16[128,768]{1,0:T(8,128)(2,1)S(1)}, bf16[128,768]{1,0:T(8,128)(2,1)S(1)}, u32[]{:S(2)}, u32[]{:S(2)}) %collective-permute-start.59) | collective-permute-done | bytes 196640 | tf_op jit(solution)/shard_map/ppermute | solution.py:76
  288.6 3.4 %collective-permute-done.61 = f32[4,1024]{1,0:T(4,128)S(1)} collective-permute-done((f32[4,1024]{1,0:T(4,128)S(1)}, f32[4,1024]{1,0:T(4,128)S(1)}, u32[]{:S(2)}, u32[]{:S(2)}) %collective-permute-start.61) | collective-permute-done | bytes 16416 | tf_op jit(solution)/shard_map/ppermute | solution.py:25
  295.8 3.7 %collective-permute-done.62.three_ref = bf16[128,768]{1,0:T(8,128)(2,1)S(1)} collective-permute-done((bf16[128,768]{1,0:T(8,128)(2,1)S(1)}, bf16[128,768]{1,0:T(8,128)(2,1)S(1)}, u32[]{:S(2)}, u32[]{:S(2)}) %collective-permute-start.62) | collective-permute-done | bytes 196640 | tf_op jit(solution)/shard_map/ppermute | solution.py:76
  (367 shorter events, 141.0 us)
Async XLA Ops:
  23.7 19.1 %collective-permute-start.13 = (bf16[272,1024]{1,0:T(8,128)(2,1)S(1)}, bf16[272,1024]{1,0:T(8,128)(2,1)}, u32[]{:S(2)}, u32[]{:S(2)}) collective-permute-start(bf16[272,1024]{1,0:T(8,128)(2,1)S(1)} %shard_map.206.refs_0_), channel_id=1, source_target_pairs={{0,2},{1,3},{2,0},{3,1},{4,6},{5,7},{6,4},{7,5},{8,10},{9,11},{10,... | collective-permute-start | bytes 1671176 | tf_op jit(solution)/shard_map/ppermute | solution.py:25
  43.0 30.5 %collective-permute-start.19 = (bf16[256,1024]{1,0:T(8,128)(2,1)}, bf16[256,1024]{1,0:T(8,128)(2,1)}, u32[]{:S(2)}, u32[]{:S(2)}) collective-permute-start(bf16[256,1024]{1,0:T(8,128)(2,1)} %shard_map.207.refs_4_), channel_id=1, source_target_pairs={{0,2},{1,3},{2,0},{3,1},{4,6},{5,7},{6,4},{7,5},{8,10},{9,11},{10,... | collective-permute-start | bytes 1572872 | tf_op jit(solution)/shard_map/ppermute | solution.py:25
  43.4 30.1 %collective-permute-start.18 = (bf16[256,1024]{1,0:T(8,128)(2,1)}, bf16[256,1024]{1,0:T(8,128)(2,1)}, u32[]{:S(2)}, u32[]{:S(2)}) collective-permute-start(bf16[256,1024]{1,0:T(8,128)(2,1)} %shard_map.207.refs_4_), channel_id=1, source_target_pairs={{0,1},{1,0},{2,3},{3,2},{4,5},{5,4},{6,7},{7,6},{8,9},{9,8},{10,11... | collective-permute-start | bytes 1572872 | tf_op jit(solution)/shard_map/ppermute | solution.py:25
  51.0 22.5 %collective-permute-start.17 = (bf16[128,3456]{1,0:T(8,128)(2,1)}, bf16[128,3456]{1,0:T(8,128)(2,1)}, u32[]{:S(2)}, u32[]{:S(2)}) collective-permute-start(bf16[128,3456]{1,0:T(8,128)(2,1)} %shard_map.208.refs_8_), channel_id=1, source_target_pairs={{0,4},{4,0},{8,12},{12,8},{16,20},{20,16},{24,28},{28,24},{1,5},{5... | collective-permute-start | bytes 2654216 | tf_op jit(solution)/shard_map/ppermute | solution.py:25
  52.7 23.0 %collective-permute-start.16 = (bf16[128,3456]{1,0:T(8,128)(2,1)}, bf16[128,3456]{1,0:T(8,128)(2,1)}, u32[]{:S(2)}, u32[]{:S(2)}) collective-permute-start(bf16[128,3456]{1,0:T(8,128)(2,1)} %shard_map.208.refs_8_), channel_id=1, source_target_pairs={{0,8},{4,12},{8,16},{12,20},{16,24},{20,28},{24,0},{28,4},{1,9},{5... | collective-permute-start | bytes 2654216 | tf_op jit(solution)/shard_map/ppermute | solution.py:76
  75.7 20.2 %collective-permute-start.23 = (bf16[128,3456]{1,0:T(8,128)(2,1)}, bf16[128,3456]{1,0:T(8,128)(2,1)S(1)}, u32[]{:S(2)}, u32[]{:S(2)}) collective-permute-start(bf16[128,3456]{1,0:T(8,128)(2,1)} %collective-permute-done.16.refs_9_), channel_id=1, source_target_pairs={{0,4},{4,0},{8,12},{12,8},{16,20},{20,16},{24,28},{28,24},{1,5},{5... | collective-permute-start | bytes 2654216 | tf_op jit(solution)/shard_map/ppermute | solution.py:25
  76.0 21.7 %collective-permute-start.22 = (bf16[128,3456]{1,0:T(8,128)(2,1)}, bf16[128,3456]{1,0:T(8,128)(2,1)S(1)}, u32[]{:S(2)}, u32[]{:S(2)}) collective-permute-start(bf16[128,3456]{1,0:T(8,128)(2,1)} %collective-permute-done.16.refs_9_), channel_id=1, source_target_pairs={{0,8},{4,12},{8,16},{12,20},{16,24},{20,28},{24,0},{28,4},{1,9},{5... | collective-permute-start | bytes 2654216 | tf_op jit(solution)/shard_map/ppermute | solution.py:76
  99.4 18.5 %collective-permute-start.28 = (bf16[128,3456]{1,0:T(8,128)(2,1)S(1)}, bf16[128,3456]{1,0:T(8,128)(2,1)S(1)}, u32[]{:S(2)}, u32[]{:S(2)}) collective-permute-start(bf16[128,3456]{1,0:T(8,128)(2,1)S(1)} %collective-permute-done.22.refs_10_), channel_id=1, source_target_pairs={{0,4},{4,0},{8,12},{12,8},{16,20},{20,16},{24,28},{28,24},{1,5},{5... | collective-permute-start | bytes 2654216 | tf_op jit(solution)/shard_map/ppermute | solution.py:25
  100.9 20.0 %collective-permute-start.27 = (bf16[128,3456]{1,0:T(8,128)(2,1)S(1)}, bf16[128,3456]{1,0:T(8,128)(2,1)S(1)}, u32[]{:S(2)}, u32[]{:S(2)}) collective-permute-start(bf16[128,3456]{1,0:T(8,128)(2,1)S(1)} %collective-permute-done.22.refs_10_), channel_id=1, source_target_pairs={{0,8},{4,12},{8,16},{12,20},{16,24},{20,28},{24,0},{28,4},{1,9},{5... | collective-permute-start | bytes 2654216 | tf_op jit(solution)/shard_map/ppermute | solution.py:76
  120.9 14.7 %collective-permute-start.29 = (bf16[256,1024]{1,0:T(8,128)(2,1)S(1)}, bf16[256,1024]{1,0:T(8,128)(2,1)S(1)}, u32[]{:S(2)}, u32[]{:S(2)}) collective-permute-start(bf16[256,1024]{1,0:T(8,128)(2,1)S(1)} %collective-permute-done.26.refs_2_), channel_id=1, source_target_pairs={{0,1},{1,0},{2,3},{3,2},{4,5},{5,4},{6,7},{7,6},{8,9},{9,8},{10,11... | collective-permute-start | bytes 1572872 | tf_op jit(solution)/shard_map/ppermute | solution.py:25
  177.7 20.1 %collective-permute-start.43 = (bf16[128,3456]{1,0:T(8,128)(2,1)S(1)}, bf16[128,3456]{1,0:T(8,128)(2,1)S(1)}, u32[]{:S(2)}, u32[]{:S(2)}) collective-permute-start(bf16[128,3456]{1,0:T(8,128)(2,1)S(1)} %pad_maximum_fusion.4), channel_id=1, source_target_pairs={{0,4},{4,0},{8,12},{12,8},{16,20},{20,16},{24,28},{28,24},{1,5},{5... | collective-permute-start | bytes 2654216 | tf_op jit(solution)/shard_map/ppermute | solution.py:25
  179.2 21.6 %collective-permute-start.44 = (bf16[128,3456]{1,0:T(8,128)(2,1)S(1)}, bf16[128,3456]{1,0:T(8,128)(2,1)S(1)}, u32[]{:S(2)}, u32[]{:S(2)}) collective-permute-start(bf16[128,3456]{1,0:T(8,128)(2,1)S(1)} %pad_maximum_fusion.2), channel_id=1, source_target_pairs={{0,8},{4,12},{8,16},{12,20},{16,24},{20,28},{24,0},{28,4},{1,9},{5... | collective-permute-start | bytes 2654216 | tf_op jit(solution)/shard_map/ppermute | solution.py:76
  191.7 19.2 %collective-permute-start.40 = (bf16[256,1024]{1,0:T(8,128)(2,1)}, bf16[256,1024]{1,0:T(8,128)(2,1)}, u32[]{:S(2)}, u32[]{:S(2)}) collective-permute-start(bf16[256,1024]{1,0:T(8,128)(2,1)} %get-tuple-element.248.refs_2_), channel_id=1, source_target_pairs={{0,1},{1,0},{2,3},{3,2},{4,5},{5,4},{6,7},{7,6},{8,9},{9,8},{10,11... | collective-permute-start | bytes 1572872 | tf_op jit(solution)/shard_map/ppermute | solution.py:25
  191.7 14.6 %collective-permute-start.38 = (bf16[256,1024]{1,0:T(8,128)(2,1)}, bf16[256,1024]{1,0:T(8,128)(2,1)}, u32[]{:S(2)}, u32[]{:S(2)}) collective-permute-start(bf16[256,1024]{1,0:T(8,128)(2,1)} %get-tuple-element.248.refs_2_), channel_id=1, source_target_pairs={{0,2},{1,3},{2,0},{3,1},{4,6},{5,7},{6,4},{7,5},{8,10},{9,11},{10,... | collective-permute-start | bytes 1572872 | tf_op jit(solution)/shard_map/ppermute | solution.py:25
  202.0 36.3 %collective-permute-start.49 = (bf16[128,3456]{1,0:T(8,128)(2,1)}, bf16[128,3456]{1,0:T(8,128)(2,1)}, u32[]{:S(2)}, u32[]{:S(2)}) collective-permute-start(bf16[128,3456]{1,0:T(8,128)(2,1)} %pad_maximum_fusion.5), channel_id=1, source_target_pairs={{0,4},{4,0},{8,12},{12,8},{16,20},{20,16},{24,28},{28,24},{1,5},{5... | collective-permute-start | bytes 2654216 | tf_op jit(solution)/shard_map/ppermute | solution.py:25
  202.6 35.7 %collective-permute-start.50 = (bf16[128,3456]{1,0:T(8,128)(2,1)}, bf16[128,3456]{1,0:T(8,128)(2,1)}, u32[]{:S(2)}, u32[]{:S(2)}) collective-permute-start(bf16[128,3456]{1,0:T(8,128)(2,1)} %add_convert_fusion.1.refs_0_), channel_id=1, source_target_pairs={{0,8},{4,12},{8,16},{12,20},{16,24},{20,28},{24,0},{28,4},{1,9},{5... | collective-permute-start | bytes 2654216 | tf_op jit(solution)/shard_map/ppermute | solution.py:76
  208.6 58.5 %collective-permute-start.39 = (bf16[256,1024]{1,0:T(8,128)(2,1)}, bf16[256,1024]{1,0:T(8,128)(2,1)S(1)}, u32[]{:S(2)}, u32[]{:S(2)}) collective-permute-start(bf16[256,1024]{1,0:T(8,128)(2,1)} %copy-done.54), channel_id=1, source_target_pairs={{0,1},{1,0},{2,3},{3,2},{4,5},{5,4},{6,7},{7,6},{8,9},{9,8},{10,11... | collective-permute-start | bytes 1572872 | tf_op jit(solution)/shard_map/ppermute | solution.py:25
  238.3 25.9 %collective-permute-start.55 = (bf16[128,3456]{1,0:T(8,128)(2,1)S(1)}, bf16[128,3456]{1,0:T(8,128)(2,1)S(1)}, u32[]{:S(2)}, u32[]{:S(2)}) collective-permute-start(bf16[128,3456]{1,0:T(8,128)(2,1)S(1)} %copy-done.76), channel_id=1, source_target_pairs={{0,4},{4,0},{8,12},{12,8},{16,20},{20,16},{24,28},{28,24},{1,5},{5... | collective-permute-start | bytes 2654216 | tf_op jit(solution)/shard_map/ppermute | solution.py:25
  240.2 25.7 %collective-permute-start.56 = (bf16[128,3456]{1,0:T(8,128)(2,1)S(1)}, bf16[128,3456]{1,0:T(8,128)(2,1)S(1)}, u32[]{:S(2)}, u32[]{:S(2)}) collective-permute-start(bf16[128,3456]{1,0:T(8,128)(2,1)S(1)} %add_convert_fusion), channel_id=1, source_target_pairs={{0,8},{4,12},{8,16},{12,20},{16,24},{20,28},{24,0},{28,4},{1,9},{5... | collective-permute-start | bytes 2654216 | tf_op jit(solution)/shard_map/ppermute | solution.py:76
  241.3 27.3 %collective-permute-start.45 = (bf16[256,1024]{1,0:T(8,128)(2,1)}, bf16[256,1024]{1,0:T(8,128)(2,1)}, u32[]{:S(2)}, u32[]{:S(2)}) collective-permute-start(bf16[256,1024]{1,0:T(8,128)(2,1)} %add_convert_fusion.3), channel_id=1, source_target_pairs={{0,2},{1,3},{2,0},{3,1},{4,6},{5,7},{6,4},{7,5},{8,10},{9,11},{10,... | collective-permute-start | bytes 1572872 | tf_op jit(solution)/shard_map/ppermute | solution.py:25
  245.9 18.2 %collective-permute-start.54 = (bf16[128,768]{1,0:T(8,128)(2,1)S(1)}, bf16[128,768]{1,0:T(8,128)(2,1)S(1)}, u32[]{:S(2)}, u32[]{:S(2)}) collective-permute-start(bf16[128,768]{1,0:T(8,128)(2,1)S(1)} %get-tuple-element.276), channel_id=1, source_target_pairs={{0,4},{4,0},{8,12},{12,8},{16,20},{20,16},{24,28},{28,24},{1,5},{5... | collective-permute-start | bytes 589832 | tf_op jit(solution)/shard_map/ppermute | solution.py:25
  264.2 16.6 %collective-permute-start.46 = (bf16[256,1024]{1,0:T(8,128)(2,1)}, bf16[256,1024]{1,0:T(8,128)(2,1)S(1)}, u32[]{:S(2)}, u32[]{:S(2)}) collective-permute-start(bf16[256,1024]{1,0:T(8,128)(2,1)} %get-tuple-element.260), channel_id=1, source_target_pairs={{0,1},{1,0},{2,3},{3,2},{4,5},{5,4},{6,7},{7,6},{8,9},{9,8},{10,11... | collective-permute-start | bytes 1572872 | tf_op jit(solution)/shard_map/ppermute | solution.py:25
  265.1 15.6 %collective-permute-start.48 = (bf16[256,1024]{1,0:T(8,128)(2,1)}, bf16[256,1024]{1,0:T(8,128)(2,1)S(1)}, u32[]{:S(2)}, u32[]{:S(2)}) collective-permute-start(bf16[256,1024]{1,0:T(8,128)(2,1)} %add_convert_fusion.2), channel_id=1, source_target_pairs={{0,2},{1,3},{2,0},{3,1},{4,6},{5,7},{6,4},{7,5},{8,10},{9,11},{10,... | collective-permute-start | bytes 1572872 | tf_op jit(solution)/shard_map/ppermute | solution.py:25
  274.1 17.8 %collective-permute-start.51 = (bf16[128,768]{1,0:T(8,128)(2,1)S(1)}, bf16[128,768]{1,0:T(8,128)(2,1)S(1)}, u32[]{:S(2)}, u32[]{:S(2)}) collective-permute-start(bf16[128,768]{1,0:T(8,128)(2,1)S(1)} %copy-done.62), channel_id=1, source_target_pairs={{0,4},{4,0},{8,12},{12,8},{16,20},{20,16},{24,28},{28,24},{1,5},{5... | collective-permute-start | bytes 589832 | tf_op jit(solution)/shard_map/ppermute | solution.py:25
  (125 other events, 1083.7 us)
where the time goes:
time: 309 us; the launch traced here: 307 us
  waiting for transfers between devices  117 us (38%)
  Pallas kernels  76.9 us (25%)
  starting transfers between devices  46.3 us (15%)
  local copies, waits for them, and re-layouts  36.9 us (12%)
  other arithmetic  19.2 us (6%)
  matrix products  9.49 us (3%)
    pallas_call x20, Pallas kernels, call(): pl.pallas_call(body, out_shape=[jax.ShapeDtypeStruct(shape, kind) for sha...  76.4 us
    ppermute x57, waiting for transfers between devices, flip(): return lax.ppermute(value, axis, [(i, i ^ bits) for i in range(size)])  63.8 us
    ppermute x14, waiting for transfers between devices, along_z(): return lax.ppermute(value, 'dp', [(i, (i + 2) % 8) for i in range(8)])  53.1 us
    ppermute x57, starting transfers between devices, flip(): return lax.ppermute(value, axis, [(i, i ^ bits) for i in range(size)])  39.3 us
    unnamed x156, local copies, waits for them, and re-layouts  32.2 us
    dot_general x6, matrix products, dot_tn(): lax.dot_general(a, b, (((0,), (0,)), ((), ())), preferred_element_type=F32)  9.49 us
    convert_element_type x11, other arithmetic, add_low(): return total.astype(BF)  7.99 us
    ppermute x14, starting transfers between devices, along_z(): return lax.ppermute(value, 'dp', [(i, (i + 2) % 8) for i in range(8)])  6.99 us
  transfers between devices with their start and end apart: 71, of which 32 were waited for; matrix products, arithmetic and copies ran while one was open for 9% of the time, Pallas kernels for 21%

commit v1 on v0

--- a/solution.py
+++ b/solution.py
@@ -218,12 +218,12 @@
 
 def prepare_body(rows, *refs):
     packs, blocks = refs[:4], refs[4:12]
-    cos_ref, sin_ref, head_ref = refs[12:15]
-    normed_ref, qk_pre_ref, q_ref, kd_ref, vd_ref, kt_ref, vt_ref = refs[15:22]
-    wqkv_ref, wo_ref, gains_ref, all_ref = refs[22:26]
+    table_ref, head_ref = refs[12:14]
+    normed_ref, saved_ref, q_ref, kd_ref, rest_ref, kt_ref, vt_ref = refs[14:21]
+    wo_ref, gains_ref, all_ref = refs[21:24]
     for i, block in enumerate(blocks):
         at = i * LANES
-        wqkv_ref[at : at + LANES, :] = block[:LANES, :512]
+        rest_ref[at : at + LANES, 256:] = block[:LANES, :512]
         wo_ref[at : at + LANES, :] = block[:LANES, 512:]
         gains_ref[:, at : at + LANES] = block[LANES : LANES + 8, :LANES].astype(F32)
     for j, pack in enumerate(packs):
@@ -238,9 +238,10 @@
         scale = lax.rsqrt(jnp.mean(x * x, -1, keepdims=True) + EPS)
         normed = (x * scale * gain).astype(BF)
         normed_ref[at, :] = normed
-        pre = jnp.dot(normed, wqkv_ref[...], preferred_element_type=F32)
-        qk_pre_ref[at, :] = pre[:, :384]
-        cos, sin = cos_ref[at, :], sin_ref[at, :]
+        pre = jnp.dot(normed, rest_ref[:, 256:], preferred_element_type=F32)
+        saved_ref[at, :384] = pre[:, :384]
+        saved_ref[at, 384:] = table_ref[at, :]
+        cos, sin = doubled(table_ref[at, :], left)
         turned = []
         for b in range(3):
             u = pre[:, b * LANES : (b + 1) * LANES]
@@ -249,11 +250,14 @@
         q_ref[0, at, :] = turned[0].astype(BF)
         q_ref[1, at, :] = turned[1].astype(BF)
         key, value = turned[2], pre[:, 384:]
-        for both, flat, one in ((kd_ref, kt_ref, key), (vd_ref, vt_ref, value)):
-            low, high = doubled(one, left)
-            both[0, at, :] = low.astype(BF)
-            both[1, at, :] = high.astype(BF)
-            flat[:, at] = one.T.astype(BF)
+        low, high = doubled(key, left)
+        kd_ref[0, at, :] = low.astype(BF)
+        kd_ref[1, at, :] = high.astype(BF)
+        kt_ref[:, at] = key.T.astype(BF)
+        low, high = doubled(value, left)
+        rest_ref[at, :LANES] = low.astype(BF)
+        rest_ref[at, LANES:256] = high.astype(BF)
+        vt_ref[:, at] = value.T.astype(BF)
         return 0
 
     lax.fori_loop(0, all_ref.shape[0] // LANES, chunk, 0)
@@ -323,10 +327,10 @@
 def attend_back_body(rows, *refs):
     me_ref, first_ref = refs[:2]
     refs = refs[1:]
-    g0, g1, g2, g3, q_ref, kd_ref, vd_ref, kt_ref, start_ref, wide_ref, lse_ref = refs[1:12]
-    qk_pre_ref, cos_ref, sin_ref, head_ref, wqkv_ref, wo_ref, normed_ref, gains_ref = refs[12:20]
-    parts, low_ref, head_sum_ref, gain_sum_ref, grad_ref = refs[20:24], *refs[24:28]
-    mixed_ref, dq_ref, dk_ref, dv_ref, acc_ref = refs[28:33]
+    g0, g1, g2, g3, q_ref, kd_ref, rest_ref, kt_ref, start_ref, wide_ref, lse_ref = refs[1:12]
+    saved_ref, head_ref, wo_ref, normed_ref, gains_ref = refs[12:17]
+    parts, low_ref, head_sum_ref, gain_sum_ref, grad_ref = refs[17:21], *refs[21:25]
+    mixed_ref, dq_ref, dk_ref, dv_ref, acc_ref = refs[25:30]
     me = me_ref[0]
     left = lax.broadcasted_iota(jnp.int32, (rows, LANES), 1) < 64
     for j, g in enumerate((g0, g1, g2, g3)):
@@ -370,7 +374,7 @@
                 scores = dot_nt(kd_ref[kv, at_k, :], q2)
                 mask = seen(start_row, (a - d) * rows, rows, a if d == 0 else None)
                 p = jnp.where(mask, jnp.exp2(scores * SCORE - lse), 0.0)
-                gp = dot_nt(vd_ref[kv, at_k, :], g2)
+                gp = dot_nt(rest_ref[at_k, columns(kv, LANES)], g2)
                 gs = (p * (gp - inner)).astype(BF)
                 dv_ref[kv, at_k, :] += dot(p.astype(BF), g2)
                 dk_ref[kv, at_k, :] += dot(gs, q2)
@@ -392,9 +396,9 @@
 
     def chunk(i, _):
         at = pl.ds(pl.multiple_of(i * LANES, LANES), LANES)
-        cos, sin = cos_ref[at, :], sin_ref[at, :]
+        cos, sin = doubled(saved_ref[at, 384:], left)
         for b in range(3):
-            u = qk_pre_ref[at, b * LANES : (b + 1) * LANES]
+            u = saved_ref[at, b * LANES : (b + 1) * LANES]
             g = folded(dk_ref, at) * 0.125 if b == 2 else dq_ref[b, at, :]
             w = g * cos - turn(g, first) * sin
             row = 1 if b == 2 else 0
@@ -411,7 +415,7 @@
     gain_sum = jnp.zeros((1, normed_ref.shape[1]), F32)
     for j in range(4):
         at = slice(j * rows, (j + 1) * rows)
-        grad = dot_nt(low_ref[at, :], wqkv_ref[...])
+        grad = dot_nt(low_ref[at, :], rest_ref[:, 256:])
         parts[j][...] = grad.astype(BF)
         gain_sum = gain_sum + jnp.sum(grad * normed_ref[at, :].astype(F32), 0, keepdims=True)
     gain_sum_ref[...] = gain_sum / gains_ref[0:1, :]
@@ -670,29 +674,28 @@
     lane = jnp.arange(LANES)
     freqs = THETA ** (-(2.0 * (lane % half).astype(F32)) / head_dim)
     angles = positions[:, None] * freqs
-    cosine = jnp.cos(angles)
     sine = jnp.sin(angles) * jnp.where(lane % head_dim < half, -1.0, 1.0)
+    table = jnp.where(lane < head_dim, jnp.cos(angles), sine)
     starts = starts.reshape(4, local_len)
     firsts = starts[:, 0]
     starts = jnp.concatenate([starts, starts], 1).reshape(4, 1, 2 * local_len)
     head_gains = jnp.concatenate([head_norm_gains, head_norm_gains], 1).astype(F32)
 
     part_shapes = [((local_len, model_dim), BF)] * 4
-    normed_one, qk_pre, queries, keys, values, keys_t, values_t, w_qkv, wo_t, gains = call(
+    normed_one, saved, queries, keys, rest, keys_t, values_t, wo_t, gains = call(
         functools.partial(prepare_body, local_len),
         [
             ((full_len, model_dim), BF),
-            ((full_len, q_cols + kv_cols), F32),
+            ((full_len, q_cols + kv_cols + LANES), F32),
             ((2, full_len, LANES), BF),
             ((2, full_len, LANES), BF),
-            ((2, full_len, LANES), BF),
+            ((full_len, 2 * LANES + q_cols + 2 * kv_cols), BF),
             ((LANES, full_len), BF),
             ((LANES, full_len), BF),
-            ((model_dim, q_cols + 2 * kv_cols), BF),
             ((model_dim, q_cols), BF),
             ((8, model_dim), F32),
         ],
-        [*packs, *blocks, cosine, sine, head_gains],
+        [*packs, *blocks, table, head_gains],
         [pltpu.VMEM((full_len, model_dim), BF)],
         limit=28,
         flops=HEAVY,
@@ -840,7 +843,7 @@
     if fast:
         total, third = bar(add_low(near[2], second, total), far[3])
         grad_attn, down_far, tick_two = bar(grad_attn, down_far, tick(total))
-        total, third = along_z(total), across_y(third)
+        total, third, fourth = along_z(total), across_y(third), across_y(far[0])
     down_far = flip(down_far, "ctx", 4, 2)
     *one_parts, grad_qkv, head_sums, gain_one, grad_attn_all = call(
         functools.partial(attend_back_body, local_len),
@@ -857,16 +860,13 @@
             *grad_attn,
             queries,
             keys,
-            values,
+            rest,
             keys_t,
             starts,
             attn_wide,
             lse,
-            qk_pre,
-            cosine,
-            sine,
+            saved,
             head_gains,
-            w_qkv,
             wo_t,
             normed_one,
             gains,
@@ -883,8 +883,6 @@
         held=True,
     )
     if fast:
-        fourth, grad_qkv = bar(far[0], grad_qkv)
-        fourth = across_y(fourth)
         total, grad_qkv = bar(add_low(near[3], third, total), grad_qkv)
         last = (near[0], fourth, along_z(total))
     layer_out = sum_out(block_order, resid, (down_parts[0], down_near, down_far))

time: 309 us -> 306 us (level)
  local copies, waits for them, and re-layouts: 36.9 us -> 29.3 us
    ppermute x14, waiting for transfers between devices: 53.1 us -> 64.1 us  [along_z(): return lax.ppermute(value, 'dp', [(i, (i + 2) % 8) for i in range(8)])]
    ppermute x57, waiting for transfers between devices: 63.8 us -> 55.6 us  [flip(): return lax.ppermute(value, axis, [(i, i ^ bits) for i in range(size)])]
    unnamed x156 -> x134, local copies, waits for them, and re-layouts: 32.2 us -> 24.5 us
where the time goes in v1:
time: 306 us; the launch traced here: 305 us
  waiting for transfers between devices  120 us (39%)
  Pallas kernels  77.1 us (25%)
  starting transfers between devices  48.2 us (16%)
  local copies, waits for them, and re-layouts  29.3 us (10%)
  other arithmetic  19.3 us (6%)
  matrix products  9.49 us (3%)
    pallas_call x20, Pallas kernels, call(): pl.pallas_call(body, out_shape=[jax.ShapeDtypeStruct(shape, kind) for sha...  76.5 us
    ppermute x14, waiting for transfers between devices, along_z(): return lax.ppermute(value, 'dp', [(i, (i + 2) % 8) for i in range(8)])  64.1 us
    ppermute x57, waiting for transfers between devices, flip(): return lax.ppermute(value, axis, [(i, i ^ bits) for i in range(size)])  55.6 us
    ppermute x57, starting transfers between devices, flip(): return lax.ppermute(value, axis, [(i, i ^ bits) for i in range(size)])  41.1 us
    unnamed x134, local copies, waits for them, and re-layouts  24.5 us
    dot_general x6, matrix products, dot_tn(): lax.dot_general(a, b, (((0,), (0,)), ((), ())), preferred_element_type=F32)  9.49 us
    convert_element_type x11, other arithmetic, add_low(): return total.astype(BF)  8.03 us
    ppermute x14, starting transfers between devices, along_z(): return lax.ppermute(value, 'dp', [(i, (i + 2) % 8) for i in range(8)])  7.07 us
  transfers between devices with their start and end apart: 71, of which 32 were waited for; matrix products, arithmetic and copies ran while one was open for 9% of the time, Pallas kernels for 21%

profile of v1, /device:TPU:0, one launch (start us, length us, event | category | flops | bytes accessed | tf_op | source)
XLA Modules:
  0.0 304.7 jit_solution(9019336991862104714)
XLA Ops:
  18.3 4.9 %collective-permute-done.4.refs_5_ = bf16[136,768]{1,0:T(8,128)(2,1)S(1)} collective-permute-done((bf16[136,768]{1,0:T(8,128)(2,1)S(1)}, bf16[136,768]{1,0:T(8,128)(2,1)S(1)}, u32[]{:S(2)}, u32[]{:S(2)}) %collective-permute-start.4) | collective-permute-done | bytes 208928 | tf_op jit(solution)/shard_map/ppermute | solution.py:76
  29.7 6.1 %collective-permute-done.10.refs_6_ = bf16[136,768]{1,0:T(8,128)(2,1)S(1)} collective-permute-done((bf16[136,768]{1,0:T(8,128)(2,1)S(1)}, bf16[136,768]{1,0:T(8,128)(2,1)S(1)}, u32[]{:S(2)}, u32[]{:S(2)}) %collective-permute-start.10) | collective-permute-done | bytes 208928 | tf_op jit(solution)/shard_map/ppermute | solution.py:76
  39.5 4.8 %collective-permute-done.12.refs_7_ = bf16[136,768]{1,0:T(8,128)(2,1)S(1)} collective-permute-done((bf16[136,768]{1,0:T(8,128)(2,1)S(1)}, bf16[136,768]{1,0:T(8,128)(2,1)S(1)}, u32[]{:S(2)}, u32[]{:S(2)}) %collective-permute-start.12) | collective-permute-done | bytes 208928 | tf_op jit(solution)/shard_map/ppermute | solution.py:76
  47.4 5.0 %collective-permute-done.14.refs_11_ = bf16[136,768]{1,0:T(8,128)(2,1)S(1)} collective-permute-done((bf16[136,768]{1,0:T(8,128)(2,1)S(1)}, bf16[136,768]{1,0:T(8,128)(2,1)S(1)}, u32[]{:S(2)}, u32[]{:S(2)}) %collective-permute-start.14) | collective-permute-done | bytes 208928 | tf_op jit(solution)/shard_map/ppermute | solution.py:25
  56.8 8.4 %shard_map.209 = (bf16[1024,1024]{1,0:T(8,128)(2,1)S(1)}, f32[1024,512]{1,0:T(8,128)S(1)}, bf16[2,1024,128]{2,1,0:T(8,128)(2,1)S(1)}, bf16[2,1024,128]{2,1,0:T(8...) custom-call(bf16[272,1024]{1,0:T(8,128)(2,1)S(1)} %shard_map.206.ref, ...), custom_call_target="tpu_custom_call" | custom-call | flops 99999997952 | bytes 1000 | tf_op jit(solution)/shard_map/pallas_call | solution.py:117
  70.2 3.7 %collective-permute-done.17.refs_12_ = bf16[128,3456]{1,0:T(8,128)(2,1)} collective-permute-done((bf16[128,3456]{1,0:T(8,128)(2,1)}, bf16[128,3456]{1,0:T(8,128)(2,1)}, u32[]{:S(2)}, u32[]{:S(2)}) %collective-permute-start.17) | collective-permute-done | bytes 884768 | tf_op jit(solution)/shard_map/ppermute | solution.py:25
  73.8 3.2 %collective-permute-done.16.refs_9_ = bf16[128,3456]{1,0:T(8,128)(2,1)} collective-permute-done((bf16[128,3456]{1,0:T(8,128)(2,1)}, bf16[128,3456]{1,0:T(8,128)(2,1)}, u32[]{:S(2)}, u32[]{:S(2)}) %collective-permute-start.16) | collective-permute-done | bytes 884768 | tf_op jit(solution)/shard_map/ppermute | solution.py:76
  80.6 9.5 %shard_map.210 = (bf16[256,1024]{1,0:T(8,128)(2,1)S(1)}, bf16[256,1024]{1,0:T(8,128)(2,1)S(1)}, bf16[256,1024]{1,0:T(8,128)(2,1)S(1)}, bf16[256,1024]{1,0:T(8,12...) custom-call(s32[1]{0:T(128)} %bitcast.8.me_ref.refs_0_, ...), custom_call_target="tpu_custom_call" | custom-call | flops 1000000 | bytes 1000 | tf_op jit(solution)/shard_map/pallas_call | solution.py:117
  92.4 4.8 %collective-permute-done.23.refs_13_ = bf16[128,3456]{1,0:T(8,128)(2,1)S(1)} collective-permute-done((bf16[128,3456]{1,0:T(8,128)(2,1)}, bf16[128,3456]{1,0:T(8,128)(2,1)S(1)}, u32[]{:S(2)}, u32[]{:S(2)}) %collective-permute-start.23) | collective-permute-done | bytes 884768 | tf_op jit(solution)/shard_map/ppermute | solution.py:25
  102.2 8.2 %collective-permute-done.24 = bf16[256,1024]{1,0:T(8,128)(2,1)S(1)} collective-permute-done((bf16[256,1024]{1,0:T(8,128)(2,1)S(1)}, bf16[256,1024]{1,0:T(8,128)(2,1)S(1)}, u32[]{:S(2)}, u32[]{:S(2)}) %collective-permute-start.24) | collective-permute-done | bytes 524320 | tf_op jit(solution)/shard_map/ppermute | solution.py:25
  113.3 5.9 %collective-permute-done.28.refs_14_ = bf16[128,3456]{1,0:T(8,128)(2,1)S(1)} collective-permute-done((bf16[128,3456]{1,0:T(8,128)(2,1)S(1)}, bf16[128,3456]{1,0:T(8,128)(2,1)S(1)}, u32[]{:S(2)}, u32[]{:S(2)}) %collective-permute-start.28) | collective-permute-done | bytes 884768 | tf_op jit(solution)/shard_map/ppermute | solution.py:25
  123.4 13.5 %collective-permute-done.32.refs_16_ = bf16[64,3456]{1,0:T(8,128)(2,1)S(1)} collective-permute-done((bf16[64,3456]{1,0:T(8,128)(2,1)S(1)}, bf16[64,3456]{1,0:T(8,128)(2,1)S(1)}, u32[]{:S(2)}, u32[]{:S(2)}) %collective-permute-start.32) | collective-permute-done | bytes 442400 | tf_op jit(solution)/shard_map/ppermute | solution.py:76
  136.9 13.0 %shard_map.211 = (bf16[1024,1152]{1,0:T(8,128)(2,1)S(1)}, bf16[1024,1152]{1,0:T(8,128)(2,1)S(1)}, bf16[1024,1152]{1,0:T(8,128)(2,1)S(1)}, bf16[1024,2304]{1,0:T(...) custom-call(bf16[256,1024]{1,0:T(8,128)(2,1)S(1)} %multiply_convert_, ...), custom_call_target="tpu_custom_call" | custom-call | flops 1000000 | bytes 1000 | tf_op jit(solution)/shard_map/pallas_call | solution.py:117
  155.6 6.4 %shard_map.212 = (bf16[256,1024]{1,0:T(8,128)(2,1)S(1)}, bf16[256,1024]{1,0:T(8,128)(2,1)S(1)}, bf16[256,1024]{1,0:T(8,128)(2,1)S(1)}, bf16[256,1024]{1,0:T(8,128)(2,1)S(1)}) custom-call(bf16[1024,1152]{1,0:T(8,128)(2,1)S(1)} %get-tuple-element.218.gate_ref, bf16[1024,1152]{1,0:T(8,128)(2,1)S(1)} %get-tuple-element.219.up_ref, ...), custom_call_target="tpu_custom_call" | custom-call | flops 1000000 | bytes 1000 | tf_op jit(solution)/shard_map/pallas_call | solution.py:117
  163.4 5.7 %collective-permute-done.36 = bf16[64,3456]{1,0:T(8,128)(2,1)S(1)} collective-permute-done((bf16[64,3456]{1,0:T(8,128)(2,1)S(1)}, bf16[64,3456]{1,0:T(8,128)(2,1)S(1)}, u32[]{:S(2)}, u32[]{:S(2)}) %collective-permute-start.36) | collective-permute-done | bytes 442400 | tf_op jit(solution)/shard_map/ppermute | solution.py:76
  181.7 4.5 %shard_map.213 = (bf16[256,1024]{1,0:T(8,128)(2,1)S(1)}, bf16[256,1024]{1,0:T(8,128)(2,1)S(1)}, bf16[256,1024]{1,0:T(8,128)(2,1)S(1)}, bf16[256,1024]{1,0:T(8,128)(2,1)}) custom-call(bf16[1024,1152]{1,0:T(8,128)(2,1)S(1)} %get-tuple-element.229.hidden_ref, bf16[1024,1152]{1,0:T(8,128)(2,1)S(1)} %get-tuple-element.231.down_ref), custom_call_target="tpu_custom_call" | custom-call | flops 1000000 | bytes 1000 | tf_op jit(solution)/shard_map/pallas_call | solution.py:117
  186.2 3.7 %collective-permute-done.37 = bf16[256,1024]{1,0:T(8,128)(2,1)S(1)} collective-permute-done((bf16[256,1024]{1,0:T(8,128)(2,1)S(1)}, bf16[256,1024]{1,0:T(8,128)(2,1)S(1)}, u32[]{:S(2)}, u32[]{:S(2)}) %collective-permute-start.37) | collective-permute-done | bytes 524320 | tf_op jit(solution)/shard_map/ppermute | solution.py:25
  193.9 5.3 %collective-permute-done.43 = bf16[128,3456]{1,0:T(8,128)(2,1)S(1)} collective-permute-done((bf16[128,3456]{1,0:T(8,128)(2,1)S(1)}, bf16[128,3456]{1,0:T(8,128)(2,1)S(1)}, u32[]{:S(2)}, u32[]{:S(2)}) %collective-permute-start.43) | collective-permute-done | bytes 884768 | tf_op jit(solution)/shard_map/ppermute | solution.py:25
  204.0 3.7 %collective-permute-done.38.refs_4_ = bf16[256,1024]{1,0:T(8,128)(2,1)} collective-permute-done((bf16[256,1024]{1,0:T(8,128)(2,1)}, bf16[256,1024]{1,0:T(8,128)(2,1)}, u32[]{:S(2)}, u32[]{:S(2)}) %collective-permute-start.38) | collective-permute-done | bytes 524320 | tf_op jit(solution)/shard_map/ppermute | solution.py:25
  217.2 20.0 %shard_map.216 = (bf16[256,1024]{1,0:T(8,128)(2,1)S(1)}, bf16[256,1024]{1,0:T(8,128)(2,1)}, bf16[256,1024]{1,0:T(8,128)(2,1)S(1)}, bf16[256,1024]{1,0:T(8,128)(2...) custom-call(s32[1]{0:T(128)} %bitcast.8.me_ref.refs_0_, ...), custom_call_target="tpu_custom_call" | custom-call | flops 1000000 | bytes 1000 | tf_op jit(solution)/shard_map/pallas_call | solution.py:117
  242.3 3.5 %shard_map.218 = (bf16[128,768]{1,0:T(8,128)(2,1)S(1)}, bf16[128,768]{1,0:T(8,128)(2,1)S(1)}, bf16[128,768]{1,0:T(8,128)(2,1)S(1)}, bf16[128,768]{1,0:T(8,128)(2...) custom-call(bf16[1024,1024]{1,0:T(8,128)(2,1)S(1)} %get-tuple-elemen, ...), custom_call_target="tpu_custom_call" | custom-call | flops 1000000 | bytes 1000 | tf_op jit(solution)/shard_map/pallas_call | solution.py:117
  248.4 4.1 %collective-permute-done.54 = bf16[128,768]{1,0:T(8,128)(2,1)S(1)} collective-permute-done((bf16[128,768]{1,0:T(8,128)(2,1)S(1)}, bf16[128,768]{1,0:T(8,128)(2,1)S(1)}, u32[]{:S(2)}, u32[]{:S(2)}) %collective-permute-start.54) | collective-permute-done | bytes 196640 | tf_op jit(solution)/shard_map/ppermute | solution.py:25
  253.1 10.1 %collective-permute-done.56.three_ref = bf16[128,3456]{1,0:T(8,128)(2,1)S(1)} collective-permute-done((bf16[128,3456]{1,0:T(8,128)(2,1)S(1)}, bf16[128,3456]{1,0:T(8,128)(2,1)S(1)}, u32[]{:S(2)}, u32[]{:S(2)}) %collective-permute-start.56) | collective-permute-done | bytes 884768 | tf_op jit(solution)/shard_map/ppermute | solution.py:76
  285.4 3.1 %collective-permute-done.61 = f32[4,1024]{1,0:T(4,128)S(1)} collective-permute-done((f32[4,1024]{1,0:T(4,128)S(1)}, f32[4,1024]{1,0:T(4,128)S(1)}, u32[]{:S(2)}, u32[]{:S(2)}) %collective-permute-start.61) | collective-permute-done | bytes 16416 | tf_op jit(solution)/shard_map/ppermute | solution.py:25
  (346 shorter events, 141.6 us)
Async XLA Ops:
  23.7 20.6 %collective-permute-start.13 = (bf16[272,1024]{1,0:T(8,128)(2,1)S(1)}, bf16[272,1024]{1,0:T(8,128)(2,1)}, u32[]{:S(2)}, u32[]{:S(2)}) collective-permute-start(bf16[272,1024]{1,0:T(8,128)(2,1)S(1)} %shard_map.206.refs_0_), channel_id=1, source_target_pairs={{0,2},{1,3},{2,0},{3,1},{4,6},{5,7},{6,4},{7,5},{8,10},{9,11},{10,... | collective-permute-start | bytes 1671176 | tf_op jit(solution)/shard_map/ppermute | solution.py:25
  44.4 25.8 %collective-permute-start.19 = (bf16[256,1024]{1,0:T(8,128)(2,1)}, bf16[256,1024]{1,0:T(8,128)(2,1)}, u32[]{:S(2)}, u32[]{:S(2)}) collective-permute-start(bf16[256,1024]{1,0:T(8,128)(2,1)} %shard_map.207.refs_4_), channel_id=1, source_target_pairs={{0,2},{1,3},{2,0},{3,1},{4,6},{5,7},{6,4},{7,5},{8,10},{9,11},{10,... | collective-permute-start | bytes 1572872 | tf_op jit(solution)/shard_map/ppermute | solution.py:25
  44.8 25.4 %collective-permute-start.18 = (bf16[256,1024]{1,0:T(8,128)(2,1)}, bf16[256,1024]{1,0:T(8,128)(2,1)}, u32[]{:S(2)}, u32[]{:S(2)}) collective-permute-start(bf16[256,1024]{1,0:T(8,128)(2,1)} %shard_map.207.refs_4_), channel_id=1, source_target_pairs={{0,1},{1,0},{2,3},{3,2},{4,5},{5,4},{6,7},{7,6},{8,9},{9,8},{10,11... | collective-permute-start | bytes 1572872 | tf_op jit(solution)/shard_map/ppermute | solution.py:25
  52.4 21.5 %collective-permute-start.17 = (bf16[128,3456]{1,0:T(8,128)(2,1)}, bf16[128,3456]{1,0:T(8,128)(2,1)}, u32[]{:S(2)}, u32[]{:S(2)}) collective-permute-start(bf16[128,3456]{1,0:T(8,128)(2,1)} %shard_map.208.refs_8_), channel_id=1, source_target_pairs={{0,4},{4,0},{8,12},{12,8},{16,20},{20,16},{24,28},{28,24},{1,5},{5... | collective-permute-start | bytes 2654216 | tf_op jit(solution)/shard_map/ppermute | solution.py:25
  54.0 23.0 %collective-permute-start.16 = (bf16[128,3456]{1,0:T(8,128)(2,1)}, bf16[128,3456]{1,0:T(8,128)(2,1)}, u32[]{:S(2)}, u32[]{:S(2)}) collective-permute-start(bf16[128,3456]{1,0:T(8,128)(2,1)} %shard_map.208.refs_8_), channel_id=1, source_target_pairs={{0,8},{4,12},{8,16},{12,20},{16,24},{20,28},{24,0},{28,4},{1,9},{5... | collective-permute-start | bytes 2654216 | tf_op jit(solution)/shard_map/ppermute | solution.py:76
  77.0 20.2 %collective-permute-start.23 = (bf16[128,3456]{1,0:T(8,128)(2,1)}, bf16[128,3456]{1,0:T(8,128)(2,1)S(1)}, u32[]{:S(2)}, u32[]{:S(2)}) collective-permute-start(bf16[128,3456]{1,0:T(8,128)(2,1)} %collective-permute-done.16.refs_9_), channel_id=1, source_target_pairs={{0,4},{4,0},{8,12},{12,8},{16,20},{20,16},{24,28},{28,24},{1,5},{5... | collective-permute-start | bytes 2654216 | tf_op jit(solution)/shard_map/ppermute | solution.py:25
  77.4 21.7 %collective-permute-start.22 = (bf16[128,3456]{1,0:T(8,128)(2,1)}, bf16[128,3456]{1,0:T(8,128)(2,1)S(1)}, u32[]{:S(2)}, u32[]{:S(2)}) collective-permute-start(bf16[128,3456]{1,0:T(8,128)(2,1)} %collective-permute-done.16.refs_9_), channel_id=1, source_target_pairs={{0,8},{4,12},{8,16},{12,20},{16,24},{20,28},{24,0},{28,4},{1,9},{5... | collective-permute-start | bytes 2654216 | tf_op jit(solution)/shard_map/ppermute | solution.py:76
  100.7 18.5 %collective-permute-start.28 = (bf16[128,3456]{1,0:T(8,128)(2,1)S(1)}, bf16[128,3456]{1,0:T(8,128)(2,1)S(1)}, u32[]{:S(2)}, u32[]{:S(2)}) collective-permute-start(bf16[128,3456]{1,0:T(8,128)(2,1)S(1)} %collective-permute-done.22.refs_10_), channel_id=1, source_target_pairs={{0,4},{4,0},{8,12},{12,8},{16,20},{20,16},{24,28},{28,24},{1,5},{5... | collective-permute-start | bytes 2654216 | tf_op jit(solution)/shard_map/ppermute | solution.py:25
  102.2 20.0 %collective-permute-start.27 = (bf16[128,3456]{1,0:T(8,128)(2,1)S(1)}, bf16[128,3456]{1,0:T(8,128)(2,1)S(1)}, u32[]{:S(2)}, u32[]{:S(2)}) collective-permute-start(bf16[128,3456]{1,0:T(8,128)(2,1)S(1)} %collective-permute-done.22.refs_10_), channel_id=1, source_target_pairs={{0,8},{4,12},{8,16},{12,20},{16,24},{20,28},{24,0},{28,4},{1,9},{5... | collective-permute-start | bytes 2654216 | tf_op jit(solution)/shard_map/ppermute | solution.py:76
  122.2 14.7 %collective-permute-start.29 = (bf16[256,1024]{1,0:T(8,128)(2,1)S(1)}, bf16[256,1024]{1,0:T(8,128)(2,1)S(1)}, u32[]{:S(2)}, u32[]{:S(2)}) collective-permute-start(bf16[256,1024]{1,0:T(8,128)(2,1)S(1)} %collective-permute-done.26.refs_2_), channel_id=1, source_target_pairs={{0,1},{1,0},{2,3},{3,2},{4,5},{5,4},{6,7},{7,6},{8,9},{9,8},{10,11... | collective-permute-start | bytes 1572872 | tf_op jit(solution)/shard_map/ppermute | solution.py:25
  122.3 14.6 %collective-permute-start.32 = (bf16[64,3456]{1,0:T(8,128)(2,1)S(1)}, bf16[64,3456]{1,0:T(8,128)(2,1)S(1)}, u32[]{:S(2)}, u32[]{:S(2)}) collective-permute-start(bf16[64,3456]{1,0:T(8,128)(2,1)S(1)} %slice.152), channel_id=1, source_target_pairs={{0,8},{4,12},{8,16},{12,20},{16,24},{20,28},{24,0},{28,4},{1,9},{5... | collective-permute-start | bytes 1327112 | tf_op jit(solution)/shard_map/ppermute | solution.py:76
  179.1 20.1 %collective-permute-start.43 = (bf16[128,3456]{1,0:T(8,128)(2,1)S(1)}, bf16[128,3456]{1,0:T(8,128)(2,1)S(1)}, u32[]{:S(2)}, u32[]{:S(2)}) collective-permute-start(bf16[128,3456]{1,0:T(8,128)(2,1)S(1)} %pad_maximum_fusion.4), channel_id=1, source_target_pairs={{0,4},{4,0},{8,12},{12,8},{16,20},{20,16},{24,28},{28,24},{1,5},{5... | collective-permute-start | bytes 2654216 | tf_op jit(solution)/shard_map/ppermute | solution.py:25
  180.6 21.6 %collective-permute-start.44 = (bf16[128,3456]{1,0:T(8,128)(2,1)S(1)}, bf16[128,3456]{1,0:T(8,128)(2,1)S(1)}, u32[]{:S(2)}, u32[]{:S(2)}) collective-permute-start(bf16[128,3456]{1,0:T(8,128)(2,1)S(1)} %pad_maximum_fusion.2), channel_id=1, source_target_pairs={{0,8},{4,12},{8,16},{12,20},{16,24},{20,28},{24,0},{28,4},{1,9},{5... | collective-permute-start | bytes 2654216 | tf_op jit(solution)/shard_map/ppermute | solution.py:76
  193.1 19.9 %collective-permute-start.40 = (bf16[256,1024]{1,0:T(8,128)(2,1)}, bf16[256,1024]{1,0:T(8,128)(2,1)}, u32[]{:S(2)}, u32[]{:S(2)}) collective-permute-start(bf16[256,1024]{1,0:T(8,128)(2,1)} %get-tuple-element.245.refs_2_), channel_id=1, source_target_pairs={{0,1},{1,0},{2,3},{3,2},{4,5},{5,4},{6,7},{7,6},{8,9},{9,8},{10,11... | collective-permute-start | bytes 1572872 | tf_op jit(solution)/shard_map/ppermute | solution.py:25
  193.1 14.6 %collective-permute-start.38 = (bf16[256,1024]{1,0:T(8,128)(2,1)}, bf16[256,1024]{1,0:T(8,128)(2,1)}, u32[]{:S(2)}, u32[]{:S(2)}) collective-permute-start(bf16[256,1024]{1,0:T(8,128)(2,1)} %get-tuple-element.245.refs_2_), channel_id=1, source_target_pairs={{0,2},{1,3},{2,0},{3,1},{4,6},{5,7},{6,4},{7,5},{8,10},{9,11},{10,... | collective-permute-start | bytes 1572872 | tf_op jit(solution)/shard_map/ppermute | solution.py:25
  203.5 34.3 %collective-permute-start.49 = (bf16[128,3456]{1,0:T(8,128)(2,1)}, bf16[128,3456]{1,0:T(8,128)(2,1)}, u32[]{:S(2)}, u32[]{:S(2)}) collective-permute-start(bf16[128,3456]{1,0:T(8,128)(2,1)} %pad_maximum_fusion.5), channel_id=1, source_target_pairs={{0,4},{4,0},{8,12},{12,8},{16,20},{20,16},{24,28},{28,24},{1,5},{5... | collective-permute-start | bytes 2654216 | tf_op jit(solution)/shard_map/ppermute | solution.py:25
  204.0 33.7 %collective-permute-start.50 = (bf16[128,3456]{1,0:T(8,128)(2,1)}, bf16[128,3456]{1,0:T(8,128)(2,1)}, u32[]{:S(2)}, u32[]{:S(2)}) collective-permute-start(bf16[128,3456]{1,0:T(8,128)(2,1)} %add_convert_fusion.1.refs_0_), channel_id=1, source_target_pairs={{0,8},{4,12},{8,16},{12,20},{16,24},{20,28},{24,0},{28,4},{1,9},{5... | collective-permute-start | bytes 2654216 | tf_op jit(solution)/shard_map/ppermute | solution.py:76
  210.0 37.5 %collective-permute-start.55 = (bf16[128,3456]{1,0:T(8,128)(2,1)}, bf16[128,3456]{1,0:T(8,128)(2,1)S(1)}, u32[]{:S(2)}, u32[]{:S(2)}) collective-permute-start(bf16[128,3456]{1,0:T(8,128)(2,1)} %pad_maximum_fusion.7), channel_id=1, source_target_pairs={{0,4},{4,0},{8,12},{12,8},{16,20},{20,16},{24,28},{28,24},{1,5},{5... | collective-permute-start | bytes 2654216 | tf_op jit(solution)/shard_map/ppermute | solution.py:25
  213.0 52.4 %collective-permute-start.39 = (bf16[256,1024]{1,0:T(8,128)(2,1)}, bf16[256,1024]{1,0:T(8,128)(2,1)S(1)}, u32[]{:S(2)}, u32[]{:S(2)}) collective-permute-start(bf16[256,1024]{1,0:T(8,128)(2,1)} %copy-done.48), channel_id=1, source_target_pairs={{0,1},{1,0},{2,3},{3,2},{4,5},{5,4},{6,7},{7,6},{8,9},{9,8},{10,11... | collective-permute-start | bytes 1572872 | tf_op jit(solution)/shard_map/ppermute | solution.py:25
  239.7 23.5 %collective-permute-start.56 = (bf16[128,3456]{1,0:T(8,128)(2,1)S(1)}, bf16[128,3456]{1,0:T(8,128)(2,1)S(1)}, u32[]{:S(2)}, u32[]{:S(2)}) collective-permute-start(bf16[128,3456]{1,0:T(8,128)(2,1)S(1)} %add_convert_fusion), channel_id=1, source_target_pairs={{0,8},{4,12},{8,16},{12,20},{16,24},{20,28},{24,0},{28,4},{1,9},{5... | collective-permute-start | bytes 2654216 | tf_op jit(solution)/shard_map/ppermute | solution.py:76
  240.8 26.0 %collective-permute-start.45 = (bf16[256,1024]{1,0:T(8,128)(2,1)}, bf16[256,1024]{1,0:T(8,128)(2,1)}, u32[]{:S(2)}, u32[]{:S(2)}) collective-permute-start(bf16[256,1024]{1,0:T(8,128)(2,1)} %add_convert_fusion.3), channel_id=1, source_target_pairs={{0,2},{1,3},{2,0},{3,1},{4,6},{5,7},{6,4},{7,5},{8,10},{9,11},{10,... | collective-permute-start | bytes 1572872 | tf_op jit(solution)/shard_map/ppermute | solution.py:25
  248.4 28.9 %collective-permute-start.46 = (bf16[256,1024]{1,0:T(8,128)(2,1)}, bf16[256,1024]{1,0:T(8,128)(2,1)S(1)}, u32[]{:S(2)}, u32[]{:S(2)}) collective-permute-start(bf16[256,1024]{1,0:T(8,128)(2,1)} %get-tuple-element.256), channel_id=1, source_target_pairs={{0,1},{1,0},{2,3},{3,2},{4,5},{5,4},{6,7},{7,6},{8,9},{9,8},{10,11... | collective-permute-start | bytes 1572872 | tf_op jit(solution)/shard_map/ppermute | solution.py:25
  252.6 24.7 %collective-permute-start.48 = (bf16[256,1024]{1,0:T(8,128)(2,1)}, bf16[256,1024]{1,0:T(8,128)(2,1)S(1)}, u32[]{:S(2)}, u32[]{:S(2)}) collective-permute-start(bf16[256,1024]{1,0:T(8,128)(2,1)} %add_convert_fusion.2), channel_id=1, source_target_pairs={{0,2},{1,3},{2,0},{3,1},{4,6},{5,7},{6,4},{7,5},{8,10},{9,11},{10,... | collective-permute-start | bytes 1572872 | tf_op jit(solution)/shard_map/ppermute | solution.py:25
  270.5 18.0 %collective-permute-start.51 = (bf16[128,768]{1,0:T(8,128)(2,1)S(1)}, bf16[128,768]{1,0:T(8,128)(2,1)S(1)}, u32[]{:S(2)}, u32[]{:S(2)}) collective-permute-start(bf16[128,768]{1,0:T(8,128)(2,1)S(1)} %copy-done.52), channel_id=1, source_target_pairs={{0,4},{4,0},{8,12},{12,8},{16,20},{20,16},{24,28},{28,24},{1,5},{5... | collective-permute-start | bytes 589832 | tf_op jit(solution)/shard_map/ppermute | solution.py:25
  (114 other events, 1014.7 us)

commit v2 on v1

--- a/solution.py
+++ b/solution.py
@@ -607,6 +607,7 @@
             [((shard + 8, wide), BF)] * 4,
             [me_row, *attn_local, norm_gains],
             scalars=1,
+            limit=58,
         )
         ff_sent = call(
             functools.partial(spread_body, ff_widths),

time: 306 us -> 302 us (0.987)
  starting transfers between devices: 48.2 us -> 53 us
  local copies, waits for them, and re-layouts: 29.3 us -> 26.2 us
    ppermute x57, starting transfers between devices: 41.1 us -> 45.5 us  [flip(): return lax.ppermute(value, axis, [(i, i ^ bits) for i in range(size)])]
    ppermute x14, waiting for transfers between devices: 64.1 us -> 60.9 us  [along_z(): return lax.ppermute(value, 'dp', [(i, (i + 2) % 8) for i in range(8)])]
    unnamed x134 -> x126, local copies, waits for them, and re-layouts: 24.5 us -> 21.4 us
  transfers between devices with their start and end apart: 71 -> 71, of which waited for: 32 -> 32; matrix products, arithmetic and copies ran while one was open for 9% -> 9% of each run, Pallas kernels for 21% -> 20%
where the time goes in v2:
time: 302 us
  waiting for transfers between devices  117 us (39%)
  Pallas kernels  75.3 us (25%)
  starting transfers between devices  53 us (18%)
  local copies, waits for them, and re-layouts  26.2 us (9%)
  other arithmetic  19.3 us (6%)
  matrix products  9.49 us (3%)
    pallas_call x20, Pallas kernels, call(): pl.pallas_call(body, out_shape=[jax.ShapeDtypeStruct(shape, kind) for sha...  74.8 us
    ppermute x14, waiting for transfers between devices, along_z(): return lax.ppermute(value, 'dp', [(i, (i + 2) % 8) for i in range(8)])  60.9 us
    ppermute x57, waiting for transfers between devices, flip(): return lax.ppermute(value, axis, [(i, i ^ bits) for i in range(size)])  55.9 us
    ppermute x57, starting transfers between devices, flip(): return lax.ppermute(value, axis, [(i, i ^ bits) for i in range(size)])  45.5 us
    unnamed x126, local copies, waits for them, and re-layouts  21.4 us
    dot_general x6, matrix products, dot_tn(): lax.dot_general(a, b, (((0,), (0,)), ((), ())), preferred_element_type=F32)  9.49 us
    convert_element_type x11, other arithmetic, add_low(): return total.astype(BF)  8.02 us
    ppermute x14, starting transfers between devices, along_z(): return lax.ppermute(value, 'dp', [(i, (i + 2) % 8) for i in range(8)])  7.45 us
  transfers between devices with their start and end apart: 71, of which 32 were waited for; matrix products, arithmetic and copies ran while one was open for 9% of the time, Pallas kernels for 20%

profile of v2, /device:TPU:0, one launch (start us, length us, event | category | flops | bytes accessed | tf_op | source)
XLA Modules:
  0.0 301.8 jit_solution(3868252460979473386)
XLA Ops:
  17.0 4.8 %collective-permute-done.4.refs_5_ = bf16[136,768]{1,0:T(8,128)(2,1)S(1)} collective-permute-done((bf16[136,768]{1,0:T(8,128)(2,1)S(1)}, bf16[136,768]{1,0:T(8,128)(2,1)S(1)}, u32[]{:S(2)}, u32[]{:S(2)}) %collective-permute-start.4) | collective-permute-done | bytes 208928 | tf_op jit(solution)/shard_map/ppermute | solution.py:76
  27.5 6.0 %collective-permute-done.10.refs_6_ = bf16[136,768]{1,0:T(8,128)(2,1)S(1)} collective-permute-done((bf16[136,768]{1,0:T(8,128)(2,1)S(1)}, bf16[136,768]{1,0:T(8,128)(2,1)S(1)}, u32[]{:S(2)}, u32[]{:S(2)}) %collective-permute-start.10) | collective-permute-done | bytes 208928 | tf_op jit(solution)/shard_map/ppermute | solution.py:76
  37.2 4.2 %collective-permute-done.12.refs_7_ = bf16[136,768]{1,0:T(8,128)(2,1)S(1)} collective-permute-done((bf16[136,768]{1,0:T(8,128)(2,1)S(1)}, bf16[136,768]{1,0:T(8,128)(2,1)S(1)}, u32[]{:S(2)}, u32[]{:S(2)}) %collective-permute-start.12) | collective-permute-done | bytes 208928 | tf_op jit(solution)/shard_map/ppermute | solution.py:76
  44.8 5.1 %collective-permute-done.14.refs_11_ = bf16[136,768]{1,0:T(8,128)(2,1)S(1)} collective-permute-done((bf16[136,768]{1,0:T(8,128)(2,1)S(1)}, bf16[136,768]{1,0:T(8,128)(2,1)S(1)}, u32[]{:S(2)}, u32[]{:S(2)}) %collective-permute-start.14) | collective-permute-done | bytes 208928 | tf_op jit(solution)/shard_map/ppermute | solution.py:25
  54.4 8.4 %shard_map.209 = (bf16[1024,1024]{1,0:T(8,128)(2,1)S(1)}, f32[1024,512]{1,0:T(8,128)S(1)}, bf16[2,1024,128]{2,1,0:T(8,128)(2,1)S(1)}, bf16[2,1024,128]{2,1,0:T(8...) custom-call(bf16[272,1024]{1,0:T(8,128)(2,1)S(1)} %shard_map.206.ref, ...), custom_call_target="tpu_custom_call" | custom-call | flops 99999997952 | bytes 1000 | tf_op jit(solution)/shard_map/pallas_call | solution.py:117
  67.8 3.6 %collective-permute-done.17.refs_12_ = bf16[128,3456]{1,0:T(8,128)(2,1)} collective-permute-done((bf16[128,3456]{1,0:T(8,128)(2,1)}, bf16[128,3456]{1,0:T(8,128)(2,1)}, u32[]{:S(2)}, u32[]{:S(2)}) %collective-permute-start.17) | collective-permute-done | bytes 884768 | tf_op jit(solution)/shard_map/ppermute | solution.py:25
  71.4 3.0 %collective-permute-done.16.refs_9_ = bf16[128,3456]{1,0:T(8,128)(2,1)} collective-permute-done((bf16[128,3456]{1,0:T(8,128)(2,1)}, bf16[128,3456]{1,0:T(8,128)(2,1)}, u32[]{:S(2)}, u32[]{:S(2)}) %collective-permute-start.16) | collective-permute-done | bytes 884768 | tf_op jit(solution)/shard_map/ppermute | solution.py:76
  78.2 7.9 %shard_map.210 = (bf16[256,1024]{1,0:T(8,128)(2,1)S(1)}, bf16[256,1024]{1,0:T(8,128)(2,1)S(1)}, bf16[256,1024]{1,0:T(8,128)(2,1)S(1)}, bf16[256,1024]{1,0:T(8,12...) custom-call(s32[1]{0:T(128)} %bitcast.8.me_ref.refs_0_, ...), custom_call_target="tpu_custom_call" | custom-call | flops 1000000 | bytes 1000 | tf_op jit(solution)/shard_map/pallas_call | solution.py:117
  88.3 6.3 %collective-permute-done.23.refs_13_ = bf16[128,3456]{1,0:T(8,128)(2,1)S(1)} collective-permute-done((bf16[128,3456]{1,0:T(8,128)(2,1)}, bf16[128,3456]{1,0:T(8,128)(2,1)S(1)}, u32[]{:S(2)}, u32[]{:S(2)}) %collective-permute-start.23) | collective-permute-done | bytes 884768 | tf_op jit(solution)/shard_map/ppermute | solution.py:25
  99.3 8.8 %collective-permute-done.24 = bf16[256,1024]{1,0:T(8,128)(2,1)S(1)} collective-permute-done((bf16[256,1024]{1,0:T(8,128)(2,1)S(1)}, bf16[256,1024]{1,0:T(8,128)(2,1)S(1)}, u32[]{:S(2)}, u32[]{:S(2)}) %collective-permute-start.24) | collective-permute-done | bytes 524320 | tf_op jit(solution)/shard_map/ppermute | solution.py:25
  110.4 5.9 %collective-permute-done.28.refs_14_ = bf16[128,3456]{1,0:T(8,128)(2,1)S(1)} collective-permute-done((bf16[128,3456]{1,0:T(8,128)(2,1)S(1)}, bf16[128,3456]{1,0:T(8,128)(2,1)S(1)}, u32[]{:S(2)}, u32[]{:S(2)}) %collective-permute-start.28) | collective-permute-done | bytes 884768 | tf_op jit(solution)/shard_map/ppermute | solution.py:25
  116.2 3.0 %collective-permute-done.27.refs_11_ = bf16[128,3456]{1,0:T(8,128)(2,1)S(1)} collective-permute-done((bf16[128,3456]{1,0:T(8,128)(2,1)S(1)}, bf16[128,3456]{1,0:T(8,128)(2,1)S(1)}, u32[]{:S(2)}, u32[]{:S(2)}) %collective-permute-start.27) | collective-permute-done | bytes 884768 | tf_op jit(solution)/shard_map/ppermute | solution.py:76
  120.8 13.2 %collective-permute-done.32.refs_16_ = bf16[64,3456]{1,0:T(8,128)(2,1)S(1)} collective-permute-done((bf16[64,3456]{1,0:T(8,128)(2,1)S(1)}, bf16[64,3456]{1,0:T(8,128)(2,1)S(1)}, u32[]{:S(2)}, u32[]{:S(2)}) %collective-permute-start.32) | collective-permute-done | bytes 442400 | tf_op jit(solution)/shard_map/ppermute | solution.py:76
  134.0 13.0 %shard_map.211 = (bf16[1024,1152]{1,0:T(8,128)(2,1)S(1)}, bf16[1024,1152]{1,0:T(8,128)(2,1)S(1)}, bf16[1024,1152]{1,0:T(8,128)(2,1)S(1)}, bf16[1024,2304]{1,0:T(...) custom-call(bf16[256,1024]{1,0:T(8,128)(2,1)S(1)} %multiply_convert_, ...), custom_call_target="tpu_custom_call" | custom-call | flops 1000000 | bytes 1000 | tf_op jit(solution)/shard_map/pallas_call | solution.py:117
  152.6 6.4 %shard_map.212 = (bf16[256,1024]{1,0:T(8,128)(2,1)S(1)}, bf16[256,1024]{1,0:T(8,128)(2,1)S(1)}, bf16[256,1024]{1,0:T(8,128)(2,1)S(1)}, bf16[256,1024]{1,0:T(8,128)(2,1)S(1)}) custom-call(bf16[1024,1152]{1,0:T(8,128)(2,1)S(1)} %get-tuple-element.218.gate_ref, bf16[1024,1152]{1,0:T(8,128)(2,1)S(1)} %get-tuple-element.219.up_ref, ...), custom_call_target="tpu_custom_call" | custom-call | flops 1000000 | bytes 1000 | tf_op jit(solution)/shard_map/pallas_call | solution.py:117
  160.7 5.3 %collective-permute-done.36 = bf16[64,3456]{1,0:T(8,128)(2,1)S(1)} collective-permute-done((bf16[64,3456]{1,0:T(8,128)(2,1)S(1)}, bf16[64,3456]{1,0:T(8,128)(2,1)S(1)}, u32[]{:S(2)}, u32[]{:S(2)}) %collective-permute-start.36) | collective-permute-done | bytes 442400 | tf_op jit(solution)/shard_map/ppermute | solution.py:76
  178.7 4.5 %shard_map.213 = (bf16[256,1024]{1,0:T(8,128)(2,1)S(1)}, bf16[256,1024]{1,0:T(8,128)(2,1)S(1)}, bf16[256,1024]{1,0:T(8,128)(2,1)S(1)}, bf16[256,1024]{1,0:T(8,128)(2,1)}) custom-call(bf16[1024,1152]{1,0:T(8,128)(2,1)S(1)} %get-tuple-element.229.hidden_ref, bf16[1024,1152]{1,0:T(8,128)(2,1)S(1)} %get-tuple-element.231.down_ref), custom_call_target="tpu_custom_call" | custom-call | flops 1000000 | bytes 1000 | tf_op jit(solution)/shard_map/pallas_call | solution.py:117
  183.3 3.7 %collective-permute-done.37 = bf16[256,1024]{1,0:T(8,128)(2,1)S(1)} collective-permute-done((bf16[256,1024]{1,0:T(8,128)(2,1)S(1)}, bf16[256,1024]{1,0:T(8,128)(2,1)S(1)}, u32[]{:S(2)}, u32[]{:S(2)}) %collective-permute-start.37) | collective-permute-done | bytes 524320 | tf_op jit(solution)/shard_map/ppermute | solution.py:25
  191.1 5.3 %collective-permute-done.43 = bf16[128,3456]{1,0:T(8,128)(2,1)S(1)} collective-permute-done((bf16[128,3456]{1,0:T(8,128)(2,1)S(1)}, bf16[128,3456]{1,0:T(8,128)(2,1)S(1)}, u32[]{:S(2)}, u32[]{:S(2)}) %collective-permute-start.43) | collective-permute-done | bytes 884768 | tf_op jit(solution)/shard_map/ppermute | solution.py:25
  201.2 3.6 %collective-permute-done.38.refs_4_ = bf16[256,1024]{1,0:T(8,128)(2,1)} collective-permute-done((bf16[256,1024]{1,0:T(8,128)(2,1)}, bf16[256,1024]{1,0:T(8,128)(2,1)}, u32[]{:S(2)}, u32[]{:S(2)}) %collective-permute-start.38) | collective-permute-done | bytes 524320 | tf_op jit(solution)/shard_map/ppermute | solution.py:25
  214.7 18.1 %shard_map.216 = (bf16[256,1024]{1,0:T(8,128)(2,1)S(1)}, bf16[256,1024]{1,0:T(8,128)(2,1)}, bf16[256,1024]{1,0:T(8,128)(2,1)S(1)}, bf16[256,1024]{1,0:T(8,128)(2...) custom-call(s32[1]{0:T(128)} %bitcast.8.me_ref.refs_0_, ...), custom_call_target="tpu_custom_call" | custom-call | flops 1000000 | bytes 1000 | tf_op jit(solution)/shard_map/pallas_call | solution.py:117
  238.1 3.5 %shard_map.218 = (bf16[128,768]{1,0:T(8,128)(2,1)S(1)}, bf16[128,768]{1,0:T(8,128)(2,1)S(1)}, bf16[128,768]{1,0:T(8,128)(2,1)S(1)}, bf16[128,768]{1,0:T(8,128)(2...) custom-call(bf16[1024,1024]{1,0:T(8,128)(2,1)S(1)} %get-tuple-elemen, ...), custom_call_target="tpu_custom_call" | custom-call | flops 1000000 | bytes 1000 | tf_op jit(solution)/shard_map/pallas_call | solution.py:117
  249.7 9.3 %collective-permute-done.56.three_ref = bf16[128,3456]{1,0:T(8,128)(2,1)S(1)} collective-permute-done((bf16[128,3456]{1,0:T(8,128)(2,1)S(1)}, bf16[128,3456]{1,0:T(8,128)(2,1)S(1)}, u32[]{:S(2)}, u32[]{:S(2)}) %collective-permute-start.56) | collective-permute-done | bytes 884768 | tf_op jit(solution)/shard_map/ppermute | solution.py:76
  288.8 3.6 %collective-permute-done.62.three_ref = bf16[128,768]{1,0:T(8,128)(2,1)S(1)} collective-permute-done((bf16[128,768]{1,0:T(8,128)(2,1)S(1)}, bf16[128,768]{1,0:T(8,128)(2,1)S(1)}, u32[]{:S(2)}, u32[]{:S(2)}) %collective-permute-start.62) | collective-permute-done | bytes 196640 | tf_op jit(solution)/shard_map/ppermute | solution.py:76
  (338 shorter events, 143.5 us)
Async XLA Ops:
  21.8 19.6 %collective-permute-start.13 = (bf16[272,1024]{1,0:T(8,128)(2,1)S(1)}, bf16[272,1024]{1,0:T(8,128)(2,1)}, u32[]{:S(2)}, u32[]{:S(2)}) collective-permute-start(bf16[272,1024]{1,0:T(8,128)(2,1)S(1)} %shard_map.206.refs_0_), channel_id=1, source_target_pairs={{0,2},{1,3},{2,0},{3,1},{4,6},{5,7},{6,4},{7,5},{8,10},{9,11},{10,... | collective-permute-start | bytes 1671176 | tf_op jit(solution)/shard_map/ppermute | solution.py:25
  41.4 26.4 %collective-permute-start.19 = (bf16[256,1024]{1,0:T(8,128)(2,1)}, bf16[256,1024]{1,0:T(8,128)(2,1)}, u32[]{:S(2)}, u32[]{:S(2)}) collective-permute-start(bf16[256,1024]{1,0:T(8,128)(2,1)} %shard_map.207.refs_4_), channel_id=1, source_target_pairs={{0,2},{1,3},{2,0},{3,1},{4,6},{5,7},{6,4},{7,5},{8,10},{9,11},{10,... | collective-permute-start | bytes 1572872 | tf_op jit(solution)/shard_map/ppermute | solution.py:25
  42.3 25.4 %collective-permute-start.18 = (bf16[256,1024]{1,0:T(8,128)(2,1)}, bf16[256,1024]{1,0:T(8,128)(2,1)}, u32[]{:S(2)}, u32[]{:S(2)}) collective-permute-start(bf16[256,1024]{1,0:T(8,128)(2,1)} %shard_map.207.refs_4_), channel_id=1, source_target_pairs={{0,1},{1,0},{2,3},{3,2},{4,5},{5,4},{6,7},{7,6},{8,9},{9,8},{10,11... | collective-permute-start | bytes 1572872 | tf_op jit(solution)/shard_map/ppermute | solution.py:25
  49.9 21.5 %collective-permute-start.17 = (bf16[128,3456]{1,0:T(8,128)(2,1)}, bf16[128,3456]{1,0:T(8,128)(2,1)}, u32[]{:S(2)}, u32[]{:S(2)}) collective-permute-start(bf16[128,3456]{1,0:T(8,128)(2,1)} %shard_map.208.refs_8_), channel_id=1, source_target_pairs={{0,4},{4,0},{8,12},{12,8},{16,20},{20,16},{24,28},{28,24},{1,5},{5... | collective-permute-start | bytes 2654216 | tf_op jit(solution)/shard_map/ppermute | solution.py:25
  51.4 23.0 %collective-permute-start.16 = (bf16[128,3456]{1,0:T(8,128)(2,1)}, bf16[128,3456]{1,0:T(8,128)(2,1)}, u32[]{:S(2)}, u32[]{:S(2)}) collective-permute-start(bf16[128,3456]{1,0:T(8,128)(2,1)} %shard_map.208.refs_8_), channel_id=1, source_target_pairs={{0,8},{4,12},{8,16},{12,20},{16,24},{20,28},{24,0},{28,4},{1,9},{5... | collective-permute-start | bytes 2654216 | tf_op jit(solution)/shard_map/ppermute | solution.py:76
  74.4 20.2 %collective-permute-start.23 = (bf16[128,3456]{1,0:T(8,128)(2,1)}, bf16[128,3456]{1,0:T(8,128)(2,1)S(1)}, u32[]{:S(2)}, u32[]{:S(2)}) collective-permute-start(bf16[128,3456]{1,0:T(8,128)(2,1)} %collective-permute-done.16.refs_9_), channel_id=1, source_target_pairs={{0,4},{4,0},{8,12},{12,8},{16,20},{20,16},{24,28},{28,24},{1,5},{5... | collective-permute-start | bytes 2654216 | tf_op jit(solution)/shard_map/ppermute | solution.py:25
  74.9 21.7 %collective-permute-start.22 = (bf16[128,3456]{1,0:T(8,128)(2,1)}, bf16[128,3456]{1,0:T(8,128)(2,1)S(1)}, u32[]{:S(2)}, u32[]{:S(2)}) collective-permute-start(bf16[128,3456]{1,0:T(8,128)(2,1)} %collective-permute-done.16.refs_9_), channel_id=1, source_target_pairs={{0,8},{4,12},{8,16},{12,20},{16,24},{20,28},{24,0},{28,4},{1,9},{5... | collective-permute-start | bytes 2654216 | tf_op jit(solution)/shard_map/ppermute | solution.py:76
  97.8 18.5 %collective-permute-start.28 = (bf16[128,3456]{1,0:T(8,128)(2,1)S(1)}, bf16[128,3456]{1,0:T(8,128)(2,1)S(1)}, u32[]{:S(2)}, u32[]{:S(2)}) collective-permute-start(bf16[128,3456]{1,0:T(8,128)(2,1)S(1)} %collective-permute-done.22.refs_10_), channel_id=1, source_target_pairs={{0,4},{4,0},{8,12},{12,8},{16,20},{20,16},{24,28},{28,24},{1,5},{5... | collective-permute-start | bytes 2654216 | tf_op jit(solution)/shard_map/ppermute | solution.py:25
  99.3 20.0 %collective-permute-start.27 = (bf16[128,3456]{1,0:T(8,128)(2,1)S(1)}, bf16[128,3456]{1,0:T(8,128)(2,1)S(1)}, u32[]{:S(2)}, u32[]{:S(2)}) collective-permute-start(bf16[128,3456]{1,0:T(8,128)(2,1)S(1)} %collective-permute-done.22.refs_10_), channel_id=1, source_target_pairs={{0,8},{4,12},{8,16},{12,20},{16,24},{20,28},{24,0},{28,4},{1,9},{5... | collective-permute-start | bytes 2654216 | tf_op jit(solution)/shard_map/ppermute | solution.py:76
  119.3 14.7 %collective-permute-start.29 = (bf16[256,1024]{1,0:T(8,128)(2,1)S(1)}, bf16[256,1024]{1,0:T(8,128)(2,1)S(1)}, u32[]{:S(2)}, u32[]{:S(2)}) collective-permute-start(bf16[256,1024]{1,0:T(8,128)(2,1)S(1)} %collective-permute-done.26.refs_2_), channel_id=1, source_target_pairs={{0,1},{1,0},{2,3},{3,2},{4,5},{5,4},{6,7},{7,6},{8,9},{9,8},{10,11... | collective-permute-start | bytes 1572872 | tf_op jit(solution)/shard_map/ppermute | solution.py:25
  119.4 14.6 %collective-permute-start.32 = (bf16[64,3456]{1,0:T(8,128)(2,1)S(1)}, bf16[64,3456]{1,0:T(8,128)(2,1)S(1)}, u32[]{:S(2)}, u32[]{:S(2)}) collective-permute-start(bf16[64,3456]{1,0:T(8,128)(2,1)S(1)} %slice.152), channel_id=1, source_target_pairs={{0,8},{4,12},{8,16},{12,20},{16,24},{20,28},{24,0},{28,4},{1,9},{5... | collective-permute-start | bytes 1327112 | tf_op jit(solution)/shard_map/ppermute | solution.py:76
  176.3 20.1 %collective-permute-start.43 = (bf16[128,3456]{1,0:T(8,128)(2,1)S(1)}, bf16[128,3456]{1,0:T(8,128)(2,1)S(1)}, u32[]{:S(2)}, u32[]{:S(2)}) collective-permute-start(bf16[128,3456]{1,0:T(8,128)(2,1)S(1)} %pad_maximum_fusion.4), channel_id=1, source_target_pairs={{0,4},{4,0},{8,12},{12,8},{16,20},{20,16},{24,28},{28,24},{1,5},{5... | collective-permute-start | bytes 2654216 | tf_op jit(solution)/shard_map/ppermute | solution.py:25
  177.7 21.6 %collective-permute-start.44 = (bf16[128,3456]{1,0:T(8,128)(2,1)S(1)}, bf16[128,3456]{1,0:T(8,128)(2,1)S(1)}, u32[]{:S(2)}, u32[]{:S(2)}) collective-permute-start(bf16[128,3456]{1,0:T(8,128)(2,1)S(1)} %pad_maximum_fusion.2), channel_id=1, source_target_pairs={{0,8},{4,12},{8,16},{12,20},{16,24},{20,28},{24,0},{28,4},{1,9},{5... | collective-permute-start | bytes 2654216 | tf_op jit(solution)/shard_map/ppermute | solution.py:76
  190.1 20.2 %collective-permute-start.40 = (bf16[256,1024]{1,0:T(8,128)(2,1)}, bf16[256,1024]{1,0:T(8,128)(2,1)}, u32[]{:S(2)}, u32[]{:S(2)}) collective-permute-start(bf16[256,1024]{1,0:T(8,128)(2,1)} %get-tuple-element.245.refs_2_), channel_id=1, source_target_pairs={{0,1},{1,0},{2,3},{3,2},{4,5},{5,4},{6,7},{7,6},{8,9},{9,8},{10,11... | collective-permute-start | bytes 1572872 | tf_op jit(solution)/shard_map/ppermute | solution.py:25
  190.2 14.6 %collective-permute-start.38 = (bf16[256,1024]{1,0:T(8,128)(2,1)}, bf16[256,1024]{1,0:T(8,128)(2,1)}, u32[]{:S(2)}, u32[]{:S(2)}) collective-permute-start(bf16[256,1024]{1,0:T(8,128)(2,1)} %get-tuple-element.245.refs_2_), channel_id=1, source_target_pairs={{0,2},{1,3},{2,0},{3,1},{4,6},{5,7},{6,4},{7,5},{8,10},{9,11},{10,... | collective-permute-start | bytes 1572872 | tf_op jit(solution)/shard_map/ppermute | solution.py:25
  200.5 32.8 %collective-permute-start.49 = (bf16[128,3456]{1,0:T(8,128)(2,1)}, bf16[128,3456]{1,0:T(8,128)(2,1)}, u32[]{:S(2)}, u32[]{:S(2)}) collective-permute-start(bf16[128,3456]{1,0:T(8,128)(2,1)} %pad_maximum_fusion.5), channel_id=1, source_target_pairs={{0,4},{4,0},{8,12},{12,8},{16,20},{20,16},{24,28},{28,24},{1,5},{5... | collective-permute-start | bytes 2654216 | tf_op jit(solution)/shard_map/ppermute | solution.py:25
  201.2 32.1 %collective-permute-start.50 = (bf16[128,3456]{1,0:T(8,128)(2,1)}, bf16[128,3456]{1,0:T(8,128)(2,1)}, u32[]{:S(2)}, u32[]{:S(2)}) collective-permute-start(bf16[128,3456]{1,0:T(8,128)(2,1)} %add_convert_fusion.1.refs_0_), channel_id=1, source_target_pairs={{0,8},{4,12},{8,16},{12,20},{16,24},{20,28},{24,0},{28,4},{1,9},{5... | collective-permute-start | bytes 2654216 | tf_op jit(solution)/shard_map/ppermute | solution.py:76
  207.1 37.6 %collective-permute-start.55 = (bf16[128,3456]{1,0:T(8,128)(2,1)}, bf16[128,3456]{1,0:T(8,128)(2,1)S(1)}, u32[]{:S(2)}, u32[]{:S(2)}) collective-permute-start(bf16[128,3456]{1,0:T(8,128)(2,1)} %pad_maximum_fusion.7), channel_id=1, source_target_pairs={{0,4},{4,0},{8,12},{12,8},{16,20},{20,16},{24,28},{28,24},{1,5},{5... | collective-permute-start | bytes 2654216 | tf_op jit(solution)/shard_map/ppermute | solution.py:25
  210.4 52.1 %collective-permute-start.39 = (bf16[256,1024]{1,0:T(8,128)(2,1)}, bf16[256,1024]{1,0:T(8,128)(2,1)S(1)}, u32[]{:S(2)}, u32[]{:S(2)}) collective-permute-start(bf16[256,1024]{1,0:T(8,128)(2,1)} %copy-done.44), channel_id=1, source_target_pairs={{0,1},{1,0},{2,3},{3,2},{4,5},{5,4},{6,7},{7,6},{8,9},{9,8},{10,11... | collective-permute-start | bytes 1572872 | tf_op jit(solution)/shard_map/ppermute | solution.py:25
  235.2 23.7 %collective-permute-start.56 = (bf16[128,3456]{1,0:T(8,128)(2,1)S(1)}, bf16[128,3456]{1,0:T(8,128)(2,1)S(1)}, u32[]{:S(2)}, u32[]{:S(2)}) collective-permute-start(bf16[128,3456]{1,0:T(8,128)(2,1)S(1)} %add_convert_fusion), channel_id=1, source_target_pairs={{0,8},{4,12},{8,16},{12,20},{16,24},{20,28},{24,0},{28,4},{1,9},{5... | collective-permute-start | bytes 2654216 | tf_op jit(solution)/shard_map/ppermute | solution.py:76
  236.9 26.9 %collective-permute-start.45 = (bf16[256,1024]{1,0:T(8,128)(2,1)}, bf16[256,1024]{1,0:T(8,128)(2,1)}, u32[]{:S(2)}, u32[]{:S(2)}) collective-permute-start(bf16[256,1024]{1,0:T(8,128)(2,1)} %add_convert_fusion.3), channel_id=1, source_target_pairs={{0,2},{1,3},{2,0},{3,1},{4,6},{5,7},{6,4},{7,5},{8,10},{9,11},{10,... | collective-permute-start | bytes 1572872 | tf_op jit(solution)/shard_map/ppermute | solution.py:25
  245.6 27.7 %collective-permute-start.46 = (bf16[256,1024]{1,0:T(8,128)(2,1)}, bf16[256,1024]{1,0:T(8,128)(2,1)S(1)}, u32[]{:S(2)}, u32[]{:S(2)}) collective-permute-start(bf16[256,1024]{1,0:T(8,128)(2,1)} %get-tuple-element.256), channel_id=1, source_target_pairs={{0,1},{1,0},{2,3},{3,2},{4,5},{5,4},{6,7},{7,6},{8,9},{9,8},{10,11... | collective-permute-start | bytes 1572872 | tf_op jit(solution)/shard_map/ppermute | solution.py:25
  248.6 24.8 %collective-permute-start.48 = (bf16[256,1024]{1,0:T(8,128)(2,1)}, bf16[256,1024]{1,0:T(8,128)(2,1)S(1)}, u32[]{:S(2)}, u32[]{:S(2)}) collective-permute-start(bf16[256,1024]{1,0:T(8,128)(2,1)} %add_convert_fusion.2), channel_id=1, source_target_pairs={{0,2},{1,3},{2,0},{3,1},{4,6},{5,7},{6,4},{7,5},{8,10},{9,11},{10,... | collective-permute-start | bytes 1572872 | tf_op jit(solution)/shard_map/ppermute | solution.py:25
  267.6 16.9 %collective-permute-start.51 = (bf16[128,768]{1,0:T(8,128)(2,1)S(1)}, bf16[128,768]{1,0:T(8,128)(2,1)S(1)}, u32[]{:S(2)}, u32[]{:S(2)}) collective-permute-start(bf16[128,768]{1,0:T(8,128)(2,1)S(1)} %copy-done.48), channel_id=1, source_target_pairs={{0,4},{4,0},{8,12},{12,8},{16,20},{20,16},{24,28},{28,24},{1,5},{5... | collective-permute-start | bytes 589832 | tf_op jit(solution)/shard_map/ppermute | solution.py:25
  (110 other events, 1012.9 us)
